TPU v7x, 256 devices: a whole 4x4x8 slice. The times are simulated.
256 devices in a mesh: lon: 32 (over y_hi, z, core), lat: 8 (over x, y_lo).
Axes of the slice: x: 4, y: 4 (y_hi: 2, y_lo: 2; y = y_hi * 2 + y_lo), z: 8, core: 2. Of those that a mesh axis runs over, the one named last changes fastest.
Arguments:
- state: float32 [4, 32, 256, 4096], P(None, None, 'lat', 'lon'), may hold values from -6 to 6
- land_mask: int32 [256, 4096], P('lat', 'lon'), may hold values 0 or 1
- wet_levels: int32 [256, 4096], P('lat', 'lon'), may hold values from 1 to 32
Outputs:
- new_state: float32 [4, 32, 256, 4096], P(None, None, 'lat', 'lon')
All inputs are finite; a program needn't handle non-finite values. No bound on the sum of `land_mask` on one device may be relied on, other than what follows from the above.
Results may differ from a plain program's by a relative error of at most 0.00002.
Values sent between devices are 32-bit elements; how exact they have to be, the bound alone decides.
A program may use at most 128 MiB of HBM per device.

v0:
```python
import jax
import jax.numpy as jnp
from jax import lax
from jax.sharding import PartitionSpec as P

STEPS = 2


time_step = 0.1
lateral_mix = 0.5
column_mix = 0.5
gravity = 0.5
thermal = 0.2
haline = 0.8


def partner(array, axis, distance):
    return lax.ppermute(array, axis, [(i, i ^ 1 << distance) for i in range(lax.axis_size(axis))])


def padded(cells, sides, width, closed):
    for axis, dim in sides:
        count = lax.axis_size(axis)
        ends = count if closed else count - 1
        head = lax.slice_in_dim(cells, 0, width, axis=dim)
        tail = lax.slice_in_dim(cells, cells.shape[dim] - width, cells.shape[dim], axis=dim)
        cells = jnp.concatenate(
            [
                lax.ppermute(tail, axis, [(i, (i + 1) % count) for i in range(ends)]),
                cells,
                lax.ppermute(head, axis, [((i + 1) % count, i) for i in range(ends)]),
            ],
            axis=dim,
        )
    return cells


def wetness(land_mask, wet_levels, levels):
    level_ids = jnp.arange(levels, dtype=jnp.int32)[:, None, None]
    return ((land_mask[None] == 1) & (level_ids < wet_levels[None])).astype(jnp.float32)


def pressure(extended):
    density = haline * extended[1] - thermal * extended[0]
    return gravity * (jnp.cumsum(density, axis=0) - 0.5 * density)


def explicit(state, east_west, north_south, press_ew, press_ns, coriolis, wet):
    grad_x = (
        8.0 * (east_west[..., 3:-1] - east_west[..., 1:-3])
        - (east_west[..., 4:] - east_west[..., :-4])
    ) / 12.0
    grad_y = (
        8.0 * (north_south[..., 3:-1, :] - north_south[..., 1:-3, :])
        - (north_south[..., 4:, :] - north_south[..., :-4, :])
    ) / 12.0
    spread = (
        east_west[..., 3:-1]
        + east_west[..., 1:-3]
        + (north_south[..., 3:-1, :] + north_south[..., 1:-3, :])
        - 4.0 * state
    )
    east_vel = state[2]
    north_vel = state[3]
    carried = east_vel * grad_x + north_vel * grad_y
    press_x = 0.5 * (press_ew[..., 3:-1] - press_ew[..., 1:-3])
    press_y = 0.5 * (press_ns[..., 3:-1, :] - press_ns[..., 1:-3, :])
    zero = jnp.zeros_like(press_x)
    force = jnp.stack([zero, zero, coriolis * north_vel - press_x, -coriolis * east_vel - press_y])
    return (state + time_step * (lateral_mix * spread - carried + force)) * wet


def mirror_rows(top_rows):
    received = top_rows
    for flip_bit in range(lax.axis_size("lon").bit_length() - 1):
        received = partner(received, "lon", flip_bit)
    return received[:, :, ::-1, ::-1]


def per_device(state, land_mask, wet_levels):
    levels = state.shape[1]
    rows = state.shape[2]
    cols = state.shape[3]
    wet = wetness(land_mask, wet_levels, levels)
    band = lax.axis_index("lat")
    bands = lax.axis_size("lat")
    total_rows = rows * bands
    global_rows = band * rows + jnp.arange(rows, dtype=jnp.int32)
    coriolis = (0.2 + 0.8 * ((global_rows.astype(jnp.float32) + 0.5) / total_rows))[:, None]
    sign = jnp.array([1.0, 1.0, -1.0, -1.0], jnp.float32)[:, None, None, None]
    upper = jnp.concatenate([column_mix * wet[1:], jnp.zeros_like(wet[:1])], axis=0)
    lower = jnp.concatenate([jnp.zeros_like(wet[:1]), column_mix * wet[1:]], axis=0)
    centre = 1.0 + lower + upper
    is_top = band == bands - 1
    current = state * wet
    for step in range(STEPS):
        east_west = padded(current, (("lon", 3),), 2, True)
        north_south = padded(current, (("lat", 2),), 2, False)
        ghost = sign * mirror_rows(current[:, :, rows - 2 :, :])
        north_south = jnp.concatenate(
            [
                north_south[:, :, : rows + 2],
                jnp.where(is_top, ghost, north_south[:, :, rows + 2 :]),
            ],
            axis=2,
        )
        press_ew = pressure(east_west)
        press_ns = pressure(north_south)
        provisional = explicit(current, east_west, north_south, press_ew, press_ns, coriolis, wet)
        ratio_prev = jnp.zeros((rows, cols), jnp.float32)
        part_prev = jnp.zeros((4, rows, cols), jnp.float32)
        ratios = []
        parts = []
        for level in range(levels):
            denom = centre[level] + lower[level] * ratio_prev
            ratio_prev = -upper[level] / denom
            part_prev = (provisional[:, level] + lower[level] * part_prev) / denom
            ratios.append(ratio_prev)
            parts.append(part_prev)
        below = jnp.zeros((4, rows, cols), jnp.float32)
        values = [None] * levels
        for level in range(levels - 1, -1, -1):
            below = parts[level] - ratios[level] * below
            values[level] = below
        current = jnp.stack(values, axis=1)
    return current


def solution(mesh):
    placed = (P(None, None, "lat", "lon"), P("lat", "lon"), P("lat", "lon"))
    return jax.shard_map(
        per_device,
        mesh=mesh,
        in_specs=placed,
        out_specs=P(None, None, "lat", "lon"),
        check_vma=False,
    )
```

profile of v0, /device:TPU:14, one launch (start us, length us, event | category | flops | bytes accessed | tf_op | source)
XLA Modules:
  0.0 140.1 jit_solution(9149774513971609076)
XLA Ops:
  0.0 0.7 broadcast_compare_fusion
  0.7 0.8 fusion.61
  1.5 2.0 %broadcast_multiply_fusion = f32[4,32,32,128]{3,2,1,0:T(8,128)S(1)} fusion(f32[4,32,32,128]{3,2,1,0:T(8,128)} %param.4, f32[32,32,128]{2,1,0:T(8,128)S(1)} %fusion.61), kind=kLoop, calls=%fused_computation.70 | loop fusion | flops 524288 | bytes 4718592 | tf_op jit(solution)/shard_map/mul | solution.py:95
  3.5 0.8 fusion.214
  4.3 1.3 collective-permute-start.8
  5.6 5.2 %collective-permute-start.7 = (f32[4,32,2,128]{3,2,1,0:T(2,128)}, f32[4,32,2,128]{3,2,1,0:T(2,128)}, u32[]{:S(2)}, u32[]{:S(2)}) collective-permute-start(f32[4,32,2,128]{3,2,1,0:T(2,128)} %get-tuple-element.126), channel_id=1, source_target_pairs={{1,0},{2,1},{3,2},{4,3},{5,4},{6,5},{7,6},{9,8},{10,9},{11,10},{12... | collective-permute-start | bytes 393224 | tf_op jit(solution)/shard_map/ppermute | solution.py:31
  10.9 2.8 %fusion.213 = (f32[4,32,32,2]{3,2,1,0:T(8,128)}, f32[4,32,32,2]{3,2,1,0:T(8,128)}) fusion(f32[4,32,32,128]{3,2,1,0:T(8,128)S(1)} %broadcast_multiply_fusion), kind=kLoop, calls=%fused_computation.518 | loop fusion | bytes 131072 | tf_op jit(solution)/shard_map/slice | solution.py:25
  13.6 3.1 %copy.5 = f32[4,32,32,2]{2,1,3,0:T(8,128)} copy(f32[4,32,32,2]{3,2,1,0:T(8,128)} %get-tuple-element.124) | data formatting | bytes 65536 | tf_op jit(solution)/shard_map/slice | solution.py:25
  16.8 7.1 %collective-permute-start = (f32[4,32,32,2]{2,1,3,0:T(8,128)}, f32[4,32,32,2]{2,1,3,0:T(8,128)}, u32[]{:S(2)}, u32[]{:S(2)}) collective-permute-start(f32[4,32,32,2]{2,1,3,0:T(8,128)} %copy.5), channel_id=1, source_target_pairs={{8,0},{16,8},{24,16},{32,24},{40,32},{48,40},{56,48},{64,56},{72,6... | collective-permute-start | bytes 98312 | tf_op jit(solution)/shard_map/ppermute | solution.py:31
  23.9 3.1 %copy.7 = f32[4,32,32,2]{2,1,3,0:T(8,128)} copy(f32[4,32,32,2]{3,2,1,0:T(8,128)} %get-tuple-element.125) | data formatting | bytes 65536 | tf_op jit(solution)/shard_map/slice | solution.py:26
  27.1 0.7 slice_bitcast_fusion.34
  28.2 0.6 copy-done.6
  28.8 0.6 copy-done.9
  29.4 0.6 copy-done.12
  30.0 0.6 copy-done.15
  30.7 0.4 copy-done.18
  31.1 0.6 fusion.180
  31.8 5.1 %collective-permute-done.3 = f32[4,32,2,128]{3,2,1,0:T(2,128)S(1)} collective-permute-done((f32[4,32,2,128]{3,2,1,0:T(2,128)S(1)}, f32[4,32,2,128]{3,2,1,0:T(2,128)S(1)}, u32[]{:S(2)}, u32[]{:S(2)}) %collective-permute-start.3) | collective-permute-done | bytes 131104 | tf_op jit(solution)/shard_map/ppermute | solution.py:18
  36.9 0.7 fusion.177
  37.6 5.7 %collective-permute-done.4 = f32[4,32,2,128]{3,2,1,0:T(2,128)} collective-permute-done((f32[4,32,2,128]{3,2,1,0:T(2,128)S(1)}, f32[4,32,2,128]{3,2,1,0:T(2,128)}, u32[]{:S(2)}, u32[]{:S(2)}) %collective-permute-start.4) | collective-permute-done | bytes 131104 | tf_op jit(solution)/shard_map/ppermute | solution.py:18
  43.2 4.0 %collective-permute-start.5 = (f32[4,32,2,128]{3,2,1,0:T(2,128)}, f32[4,32,2,128]{3,2,1,0:T(2,128)}, u32[]{:S(2)}, u32[]{:S(2)}) collective-permute-start(f32[4,32,2,128]{3,2,1,0:T(2,128)} %collective-permute-done.4), channel_id=1, source_target_pairs={{0,64},{8,72},{16,80},{24,88},{32,96},{40,104},{48,112},{56,120},{... | collective-permute-start | bytes 393224 | tf_op jit(solution)/shard_map/ppermute | solution.py:18
  47.2 0.7 slice_bitcast_fusion.22
  47.9 0.6 multiply_add_fusion
  48.5 0.5 pad.19.clone
  49.0 3.0 %copy.6 = f32[4,32,32,2]{3,2,1,0:T(8,128)} copy(f32[4,32,32,2]{2,1,3,0:T(8,128)} %collective-permute-done) | data formatting | bytes 65536 | tf_op jit(solution)/shard_map/ppermute | solution.py:31
  52.1 3.0 %copy.8 = f32[4,32,32,2]{3,2,1,0:T(8,128)} copy(f32[4,32,32,2]{2,1,3,0:T(8,128)} %collective-permute-done.1) | data formatting | bytes 65536 | tf_op jit(solution)/shard_map/ppermute | solution.py:29
  55.1 2.3 %collective-permute-start.6 = (f32[4,32,2,128]{3,2,1,0:T(2,128)}, f32[4,32,2,128]{3,2,1,0:T(2,128)}, u32[]{:S(2)}, u32[]{:S(2)}) collective-permute-start(f32[4,32,2,128]{3,2,1,0:T(2,128)} %collective-permute-done.5), channel_id=1, source_target_pairs={{0,128},{8,136},{16,144},{24,152},{32,160},{40,168},{48,176},{56,1... | collective-permute-start | bytes 393224 | tf_op jit(solution)/shard_map/ppermute | solution.py:18
  57.4 4.9 %subtract_multiply_fusion.1 = f32[32,32,132]{2,1,0:T(8,128)} fusion(f32[4,32,32,2]{3,2,1,0:T(8,128)} %copy.6, f32[4,32,32,128]{3,2,1,0:T(8,128)S(1)} %broadcast_multiply_fusion, f32[4,32,32,2]{3,2,1,0:T(8,128)} %copy.8), kind=kOutput, calls=%fused_computation.69 | output fusion | flops 6488064 | bytes 2703360 | tf_op jit(solution)/shard_map/jit(cumsum)/reduce_window_sum | solution.py:45
  62.2 1.4 rev.6
  63.6 0.8 multiply_select_fusion.1
  64.5 0.3 fusion.46
  64.8 0.9 copy-done.5
  65.7 0.4 fusion.62
  66.1 1.1 copy-done.1
  67.3 0.6 copy-done.3
  68.2 4.9 %fusion.28 = f32[4,32,32,128]{3,2,1,0:T(8,128)S(1)} fusion(f32[4,32,32,128]{3,2,1,0:T(8,128)S(1)} %broadcast_multiply_fusion, f32[4,32,2,128]{3,2,1,0:T(2,128)S(1)} %collective-permute-done.8, f32[4,32,2,128]{3,2,1,0:T(2,128)S(1)} %multiply_select_fusion.1, f32[4,32,32,2]{3,2,1,0:T(8,128)S(1)} %copy-done.3, f32[4,32,32,2]{3,2,1,0:T(8,128)S(1)} %copy-done.1, ...), kind=kLoop, calls=%fused_computation.49 | loop fusion | flops 16777216 | bytes 7143440 | tf_op jit(solution)/shard_map/mul | solution.py:70
  73.5 1.6 %constant_dynamic-update-slice_fusion.31 = (f32[4,32,32,128]{3,2,1,0:T(8,128)S(1)}, f32[4,1,32,128]{3,2,1,0:T(8,128)S(1)}, f32[4,1,32,128]{3,2,1,0:T(8,128)S(1)}...) fusion(f32[32,128]{1,0:T(8,128)} %get-tuple-element.164, ...), kind=kLoop, calls=%fused_computation.151 | loop fusion | flops 2572287 | bytes 5685248
  75.7 0.8 fusion.212
  76.4 1.3 collective-permute-done.11
  77.8 5.5 %collective-permute-done.12 = f32[4,32,2,128]{3,2,1,0:T(2,128)S(1)} collective-permute-done((f32[4,32,2,128]{3,2,1,0:T(2,128)S(1)}, f32[4,32,2,128]{3,2,1,0:T(2,128)S(1)}, u32[]{:S(2)}, u32[]{:S(2)}) %collective-permute-start.12) | collective-permute-done | bytes 131104 | tf_op jit(solution)/shard_map/ppermute | solution.py:18
  83.3 0.4 collective-permute-start.13
  83.8 8.1 %collective-permute-done.13 = f32[4,32,2,128]{3,2,1,0:T(2,128)} collective-permute-done((f32[4,32,2,128]{3,2,1,0:T(2,128)S(1)}, f32[4,32,2,128]{3,2,1,0:T(2,128)}, u32[]{:S(2)}, u32[]{:S(2)}) %collective-permute-start.13) | collective-permute-done | bytes 131104 | tf_op jit(solution)/shard_map/ppermute | solution.py:18
  91.9 2.5 %collective-permute-start.14 = (f32[4,32,2,128]{3,2,1,0:T(2,128)}, f32[4,32,2,128]{3,2,1,0:T(2,128)}, u32[]{:S(2)}, u32[]{:S(2)}) collective-permute-start(f32[4,32,2,128]{3,2,1,0:T(2,128)} %collective-permute-done.13), channel_id=1, source_target_pairs={{0,64},{8,72},{16,80},{24,88},{32,96},{40,104},{48,112},{56,120},{... | collective-permute-start | bytes 393224 | tf_op jit(solution)/shard_map/ppermute | solution.py:18
  94.4 2.8 %fusion.211 = (f32[4,32,32,2]{3,2,1,0:T(8,128)}, f32[4,32,32,2]{3,2,1,0:T(8,128)}) fusion(f32[4,32,32,128]{3,2,1,0:T(8,128)S(1)} %constant_dynamic-update-slice_fusion), kind=kLoop, calls=%fused_computation.516 | loop fusion | bytes 131072 | tf_op jit(solution)/shard_map/slice | solution.py:25
  97.2 2.5 %copy.11 = f32[4,32,32,2]{2,1,3,0:T(8,128)S(1)} copy(f32[4,32,32,2]{3,2,1,0:T(8,128)} %get-tuple-element.116) | data formatting | bytes 65536 | tf_op jit(solution)/shard_map/slice | solution.py:25
  99.7 2.5 %collective-permute-start.9 = (f32[4,32,32,2]{2,1,3,0:T(8,128)S(1)}, f32[4,32,32,2]{2,1,3,0:T(8,128)}, u32[]{:S(2)}, u32[]{:S(2)}) collective-permute-start(f32[4,32,32,2]{2,1,3,0:T(8,128)S(1)} %copy.11), channel_id=1, source_target_pairs={{8,0},{16,8},{24,16},{32,24},{40,32},{48,40},{56,48},{64,56},{72,6... | collective-permute-start | bytes 98312 | tf_op jit(solution)/shard_map/ppermute | solution.py:31
  102.1 3.1 %copy.13 = f32[4,32,32,2]{2,1,3,0:T(8,128)} copy(f32[4,32,32,2]{3,2,1,0:T(8,128)} %get-tuple-element.117) | data formatting | bytes 65536 | tf_op jit(solution)/shard_map/slice | solution.py:26
  105.3 1.3 collective-permute-start.17
  106.5 5.2 %collective-permute-start.16 = (f32[4,32,2,128]{3,2,1,0:T(2,128)}, f32[4,32,2,128]{3,2,1,0:T(2,128)}, u32[]{:S(2)}, u32[]{:S(2)}) collective-permute-start(f32[4,32,2,128]{3,2,1,0:T(2,128)} %get-tuple-element.118), channel_id=1, source_target_pairs={{1,0},{2,1},{3,2},{4,3},{5,4},{6,5},{7,6},{9,8},{10,9},{11,10},{12... | collective-permute-start | bytes 393224 | tf_op jit(solution)/shard_map/ppermute | solution.py:31
  111.8 3.0 %copy.12 = f32[4,32,32,2]{3,2,1,0:T(8,128)} copy(f32[4,32,32,2]{2,1,3,0:T(8,128)} %collective-permute-done.9) | data formatting | bytes 65536 | tf_op jit(solution)/shard_map/ppermute | solution.py:31
  114.9 3.0 %copy.14 = f32[4,32,32,2]{3,2,1,0:T(8,128)} copy(f32[4,32,32,2]{2,1,3,0:T(8,128)} %collective-permute-done.10) | data formatting | bytes 65536 | tf_op jit(solution)/shard_map/ppermute | solution.py:29
  117.9 1.5 %collective-permute-start.15 = (f32[4,32,2,128]{3,2,1,0:T(2,128)}, f32[4,32,2,128]{3,2,1,0:T(2,128)}, u32[]{:S(2)}, u32[]{:S(2)}) collective-permute-start(f32[4,32,2,128]{3,2,1,0:T(2,128)} %collective-permute-done.14), channel_id=1, source_target_pairs={{0,128},{8,136},{16,144},{24,152},{32,160},{40,168},{48,176},{56,1... | collective-permute-start | bytes 393224 | tf_op jit(solution)/shard_map/ppermute | solution.py:18
  119.4 4.9 %subtract_multiply_fusion = f32[32,32,132]{2,1,0:T(8,128)} fusion(f32[4,32,32,2]{3,2,1,0:T(8,128)} %copy.12, f32[4,32,32,128]{3,2,1,0:T(8,128)S(1)} %constant_dynamic-update-slice_fusion, f32[4,32,32,2]{3,2,1,0:T(8,128)} %copy.14), kind=kOutput, calls=%fused_computation.68 | output fusion | flops 6488064 | bytes 2703360 | tf_op jit(solution)/shard_map/jit(cumsum)/reduce_window_sum | solution.py:45
  124.3 0.4 collective-permute-done.15
  124.7 1.4 rev.7
  126.1 0.8 multiply_select_fusion
  127.2 0.9 copy-done.4
  128.1 0.4 fusion.64
  128.6 1.1 copy-done
  129.7 0.6 copy-done.2
  130.7 4.9 %fusion.16 = f32[4,32,32,128]{3,2,1,0:T(8,128)S(1)} fusion(f32[4,32,32,128]{3,2,1,0:T(8,128)S(1)} %constant_dynamic-update-slice_fusion, f32[4,32,2,128]{3,2,1,0:T(2,128)S(1)} %collective-permute-done.17, f32[4,32,2,128]{3,2,1,0:T(2,128)S(1)} %multiply_select_fusion, f32[4,32,32,2]{3,2,1,0:T(8,128)S(1)} %copy-done.2, f32[4,32,32,2]{3,2,1,0:T(8,128)S(1)} %copy-done, ...), kind=kLoop, calls=%fused_computation.33 | loop fusion | flops 16777216 | bytes 7143440 | tf_op jit(solution)/shard_map/mul | solution.py:70
  136.0 1.6 %constant_dynamic-update-slice_fusion.63 = (f32[4,32,32,128]{3,2,1,0:T(8,128)S(1)}, f32[4,1,32,128]{3,2,1,0:T(8,128)S(1)}, f32[4,1,32,128]{3,2,1,0:T(8,128)S(1)}...) fusion(f32[32,128]{1,0:T(8,128)} %get-tuple-element.164, ...), kind=kLoop, calls=%fused_computation.183 | loop fusion | flops 2572287 | bytes 5685248
  138.1 1.3 copy-done.90
  139.4 0.6 constant_dynamic-update-slice_fusion.32
  (276 shorter events, 2.0 us)
Async XLA Ops:
  4.3 26.3 %collective-permute-start.2 = (f32[4,32,2,128]{3,2,1,0:T(2,128)}, f32[4,32,2,128]{3,2,1,0:T(2,128)S(1)}, u32[]{:S(2)}, u32[]{:S(2)}) collective-permute-start(f32[4,32,2,128]{3,2,1,0:T(2,128)} %get-tuple-element.127), channel_id=1, source_target_pairs={{0,8},{8,0},{16,24},{24,16},{32,40},{40,32},{48,56},{56,48},{64,72... | collective-permute-start | bytes 393224 | tf_op jit(solution)/shard_map/ppermute | solution.py:18
  4.3 60.1 %collective-permute-start.8 = (f32[4,32,2,128]{3,2,1,0:T(2,128)}, f32[4,32,2,128]{3,2,1,0:T(2,128)S(1)}, u32[]{:S(2)}, u32[]{:S(2)}) collective-permute-start(f32[4,32,2,128]{3,2,1,0:T(2,128)} %get-tuple-element.127), channel_id=1, source_target_pairs={{0,1},{1,2},{2,3},{3,4},{4,5},{5,6},{6,7},{8,9},{9,10},{10,11},{11... | collective-permute-start | bytes 393224 | tf_op jit(solution)/shard_map/ppermute | solution.py:29
  5.6 58.0 %collective-permute-start.7 = (f32[4,32,2,128]{3,2,1,0:T(2,128)}, f32[4,32,2,128]{3,2,1,0:T(2,128)}, u32[]{:S(2)}, u32[]{:S(2)}) collective-permute-start(f32[4,32,2,128]{3,2,1,0:T(2,128)} %get-tuple-element.126), channel_id=1, source_target_pairs={{1,0},{2,1},{3,2},{4,3},{5,4},{6,5},{7,6},{9,8},{10,9},{11,10},{12... | collective-permute-start | bytes 393224 | tf_op jit(solution)/shard_map/ppermute | solution.py:31
  16.8 32.3 %collective-permute-start = (f32[4,32,32,2]{2,1,3,0:T(8,128)}, f32[4,32,32,2]{2,1,3,0:T(8,128)}, u32[]{:S(2)}, u32[]{:S(2)}) collective-permute-start(f32[4,32,32,2]{2,1,3,0:T(8,128)} %copy.5), channel_id=1, source_target_pairs={{8,0},{16,8},{24,16},{32,24},{40,32},{48,40},{56,48},{64,56},{72,6... | collective-permute-start | bytes 98312 | tf_op jit(solution)/shard_map/ppermute | solution.py:31
  27.0 25.0 %collective-permute-start.1 = (f32[4,32,32,2]{2,1,3,0:T(8,128)}, f32[4,32,32,2]{2,1,3,0:T(8,128)}, u32[]{:S(2)}, u32[]{:S(2)}) collective-permute-start(f32[4,32,32,2]{2,1,3,0:T(8,128)} %copy.7), channel_id=1, source_target_pairs={{0,8},{8,16},{16,24},{24,32},{32,40},{40,48},{48,56},{56,64},{64,7... | collective-permute-start | bytes 98312 | tf_op jit(solution)/shard_map/ppermute | solution.py:29
  30.6 16.6 %copy-start.21 = (f32[1,32,128]{2,1,0:T(8,128)}, f32[1,32,128]{2,1,0:T(8,128)S(1)}, u32[]{:S(2)}) copy-start(f32[1,32,128]{2,1,0:T(8,128)S(1)} %get-tuple-element.107) | copy-start | bytes 49156
  30.6 6.3 %collective-permute-start.3 = (f32[4,32,2,128]{3,2,1,0:T(2,128)S(1)}, f32[4,32,2,128]{3,2,1,0:T(2,128)S(1)}, u32[]{:S(2)}, u32[]{:S(2)}) collective-permute-start(f32[4,32,2,128]{3,2,1,0:T(2,128)S(1)} %collective-permute-done.2), channel_id=1, source_target_pairs={{0,16},{8,24},{16,0},{24,8},{32,48},{40,56},{48,32},{56,40},{64,80... | collective-permute-start | bytes 393224 | tf_op jit(solution)/shard_map/ppermute | solution.py:18
  31.8 23.3 %copy-start.24 = (f32[1,32,128]{2,1,0:T(8,128)}, f32[1,32,128]{2,1,0:T(8,128)S(1)}, u32[]{:S(2)}) copy-start(f32[1,32,128]{2,1,0:T(8,128)S(1)} %get-tuple-element.110) | copy-start | bytes 49156
  36.9 6.4 %collective-permute-start.4 = (f32[4,32,2,128]{3,2,1,0:T(2,128)S(1)}, f32[4,32,2,128]{3,2,1,0:T(2,128)}, u32[]{:S(2)}, u32[]{:S(2)}) collective-permute-start(f32[4,32,2,128]{3,2,1,0:T(2,128)S(1)} %collective-permute-done.3), channel_id=1, source_target_pairs={{0,32},{8,40},{16,48},{24,56},{32,0},{40,8},{48,16},{56,24},{64,96... | collective-permute-start | bytes 393224 | tf_op jit(solution)/shard_map/ppermute | solution.py:18
  43.2 11.9 %collective-permute-start.5 = (f32[4,32,2,128]{3,2,1,0:T(2,128)}, f32[4,32,2,128]{3,2,1,0:T(2,128)}, u32[]{:S(2)}, u32[]{:S(2)}) collective-permute-start(f32[4,32,2,128]{3,2,1,0:T(2,128)} %collective-permute-done.4), channel_id=1, source_target_pairs={{0,64},{8,72},{16,80},{24,88},{32,96},{40,104},{48,112},{56,120},{... | collective-permute-start | bytes 393224 | tf_op jit(solution)/shard_map/ppermute | solution.py:18
  55.1 7.1 %collective-permute-start.6 = (f32[4,32,2,128]{3,2,1,0:T(2,128)}, f32[4,32,2,128]{3,2,1,0:T(2,128)}, u32[]{:S(2)}, u32[]{:S(2)}) collective-permute-start(f32[4,32,2,128]{3,2,1,0:T(2,128)} %collective-permute-done.5), channel_id=1, source_target_pairs={{0,128},{8,136},{16,144},{24,152},{32,160},{40,168},{48,176},{56,1... | collective-permute-start | bytes 393224 | tf_op jit(solution)/shard_map/ppermute | solution.py:18
  67.9 5.3 %copy-start.19 = (f32[1,32,128]{2,1,0:T(8,128)S(1)}, f32[1,32,128]{2,1,0:T(8,128)}, u32[]{:S(2)}) copy-start(f32[1,32,128]{2,1,0:T(8,128)} %copy-done.18) | copy-start | bytes 49156
  67.9 5.3 %copy-start.22 = (f32[1,32,128]{2,1,0:T(8,128)S(1)}, f32[1,32,128]{2,1,0:T(8,128)}, u32[]{:S(2)}) copy-start(f32[1,32,128]{2,1,0:T(8,128)} %copy-done.21) | copy-start | bytes 49156
  67.9 5.3 %copy-start.25 = (f32[1,32,128]{2,1,0:T(8,128)S(1)}, f32[1,32,128]{2,1,0:T(8,128)}, u32[]{:S(2)}) copy-start(f32[1,32,128]{2,1,0:T(8,128)} %copy-done.24) | copy-start | bytes 49156
  67.9 5.3 %copy-start.27 = (f32[32,128]{1,0:T(8,128)S(1)}, f32[32,128]{1,0:T(8,128)}, u32[]{:S(2)}) copy-start(f32[32,128]{1,0:T(8,128)} %get-tuple-element.167) | copy-start | bytes 49156
  67.9 5.3 %copy-start.29 = (f32[32,128]{1,0:T(8,128)S(1)}, f32[32,128]{1,0:T(8,128)}, u32[]{:S(2)}) copy-start(f32[32,128]{1,0:T(8,128)} %get-tuple-element.168) | copy-start | bytes 49156
  67.9 5.3 %copy-start.31 = (f32[32,128]{1,0:T(8,128)S(1)}, f32[32,128]{1,0:T(8,128)}, u32[]{:S(2)}) copy-start(f32[32,128]{1,0:T(8,128)} %get-tuple-element.169) | copy-start | bytes 49156
  68.0 5.3 %copy-start.33 = (f32[32,128]{1,0:T(8,128)S(1)}, f32[32,128]{1,0:T(8,128)}, u32[]{:S(2)}) copy-start(f32[32,128]{1,0:T(8,128)} %get-tuple-element.170) | copy-start | bytes 49156
  68.0 5.3 %copy-start.35 = (f32[32,128]{1,0:T(8,128)S(1)}, f32[32,128]{1,0:T(8,128)}, u32[]{:S(2)}) copy-start(f32[32,128]{1,0:T(8,128)} %get-tuple-element.171) | copy-start | bytes 49156
  68.0 5.3 %copy-start.37 = (f32[32,128]{1,0:T(8,128)S(1)}, f32[32,128]{1,0:T(8,128)}, u32[]{:S(2)}) copy-start(f32[32,128]{1,0:T(8,128)} %get-tuple-element.172) | copy-start | bytes 49156
  68.0 5.3 %copy-start.39 = (f32[32,128]{1,0:T(8,128)S(1)}, f32[32,128]{1,0:T(8,128)}, u32[]{:S(2)}) copy-start(f32[32,128]{1,0:T(8,128)} %get-tuple-element.173) | copy-start | bytes 49156
  68.0 5.3 %copy-start.41 = (f32[32,128]{1,0:T(8,128)S(1)}, f32[32,128]{1,0:T(8,128)}, u32[]{:S(2)}) copy-start(f32[32,128]{1,0:T(8,128)} %get-tuple-element.174) | copy-start | bytes 49156
  68.0 5.3 %copy-start.43 = (f32[32,128]{1,0:T(8,128)S(1)}, f32[32,128]{1,0:T(8,128)}, u32[]{:S(2)}) copy-start(f32[32,128]{1,0:T(8,128)} %get-tuple-element.175) | copy-start | bytes 49156
  68.0 5.3 %copy-start.45 = (f32[32,128]{1,0:T(8,128)S(1)}, f32[32,128]{1,0:T(8,128)}, u32[]{:S(2)}) copy-start(f32[32,128]{1,0:T(8,128)} %get-tuple-element.132) | copy-start | bytes 49156
  68.0 5.3 %copy-start.47 = (f32[32,128]{1,0:T(8,128)S(1)}, f32[32,128]{1,0:T(8,128)}, u32[]{:S(2)}) copy-start(f32[32,128]{1,0:T(8,128)} %get-tuple-element.133) | copy-start | bytes 49156
  68.0 5.3 %copy-start.49 = (f32[32,128]{1,0:T(8,128)S(1)}, f32[32,128]{1,0:T(8,128)}, u32[]{:S(2)}) copy-start(f32[32,128]{1,0:T(8,128)} %get-tuple-element.134) | copy-start | bytes 49156
  68.0 5.3 %copy-start.51 = (f32[32,128]{1,0:T(8,128)S(1)}, f32[32,128]{1,0:T(8,128)}, u32[]{:S(2)}) copy-start(f32[32,128]{1,0:T(8,128)} %get-tuple-element.135) | copy-start | bytes 49156
  68.1 5.3 %copy-start.53 = (f32[32,128]{1,0:T(8,128)S(1)}, f32[32,128]{1,0:T(8,128)}, u32[]{:S(2)}) copy-start(f32[32,128]{1,0:T(8,128)} %get-tuple-element.136) | copy-start | bytes 49156
  68.1 5.3 %copy-start.55 = (f32[32,128]{1,0:T(8,128)S(1)}, f32[32,128]{1,0:T(8,128)}, u32[]{:S(2)}) copy-start(f32[32,128]{1,0:T(8,128)} %get-tuple-element.137) | copy-start | bytes 49156
  68.1 5.3 %copy-start.57 = (f32[32,128]{1,0:T(8,128)S(1)}, f32[32,128]{1,0:T(8,128)}, u32[]{:S(2)}) copy-start(f32[32,128]{1,0:T(8,128)} %get-tuple-element.138) | copy-start | bytes 49156
  68.1 5.3 %copy-start.59 = (f32[32,128]{1,0:T(8,128)S(1)}, f32[32,128]{1,0:T(8,128)}, u32[]{:S(2)}) copy-start(f32[32,128]{1,0:T(8,128)} %get-tuple-element.139) | copy-start | bytes 49156
  68.1 5.3 %copy-start.61 = (f32[32,128]{1,0:T(8,128)S(1)}, f32[32,128]{1,0:T(8,128)}, u32[]{:S(2)}) copy-start(f32[32,128]{1,0:T(8,128)} %get-tuple-element.140) | copy-start | bytes 49156
  68.1 5.3 %copy-start.63 = (f32[32,128]{1,0:T(8,128)S(1)}, f32[32,128]{1,0:T(8,128)}, u32[]{:S(2)}) copy-start(f32[32,128]{1,0:T(8,128)} %get-tuple-element.141) | copy-start | bytes 49156
  68.1 5.3 %copy-start.65 = (f32[32,128]{1,0:T(8,128)S(1)}, f32[32,128]{1,0:T(8,128)}, u32[]{:S(2)}) copy-start(f32[32,128]{1,0:T(8,128)} %get-tuple-element.142) | copy-start | bytes 49156
  68.1 5.3 %copy-start.67 = (f32[32,128]{1,0:T(8,128)S(1)}, f32[32,128]{1,0:T(8,128)}, u32[]{:S(2)}) copy-start(f32[32,128]{1,0:T(8,128)} %get-tuple-element.143) | copy-start | bytes 49156
  68.1 5.3 %copy-start.69 = (f32[32,128]{1,0:T(8,128)S(1)}, f32[32,128]{1,0:T(8,128)}, u32[]{:S(2)}) copy-start(f32[32,128]{1,0:T(8,128)} %get-tuple-element.144) | copy-start | bytes 49156
  68.1 5.3 %copy-start.71 = (f32[32,128]{1,0:T(8,128)S(1)}, f32[32,128]{1,0:T(8,128)}, u32[]{:S(2)}) copy-start(f32[32,128]{1,0:T(8,128)} %get-tuple-element.145) | copy-start | bytes 49156
  68.2 5.3 %copy-start.73 = (f32[32,128]{1,0:T(8,128)S(1)}, f32[32,128]{1,0:T(8,128)}, u32[]{:S(2)}) copy-start(f32[32,128]{1,0:T(8,128)} %get-tuple-element.146) | copy-start | bytes 49156
  68.2 5.3 %copy-start.75 = (f32[32,128]{1,0:T(8,128)S(1)}, f32[32,128]{1,0:T(8,128)}, u32[]{:S(2)}) copy-start(f32[32,128]{1,0:T(8,128)} %get-tuple-element.147) | copy-start | bytes 49156
  68.2 5.3 %copy-start.77 = (f32[32,128]{1,0:T(8,128)S(1)}, f32[32,128]{1,0:T(8,128)}, u32[]{:S(2)}) copy-start(f32[32,128]{1,0:T(8,128)} %get-tuple-element.148) | copy-start | bytes 49156
  68.2 5.3 %copy-start.79 = (f32[32,128]{1,0:T(8,128)S(1)}, f32[32,128]{1,0:T(8,128)}, u32[]{:S(2)}) copy-start(f32[32,128]{1,0:T(8,128)} %get-tuple-element.149) | copy-start | bytes 49156
  68.2 5.3 %copy-start.81 = (f32[32,128]{1,0:T(8,128)S(1)}, f32[32,128]{1,0:T(8,128)}, u32[]{:S(2)}) copy-start(f32[32,128]{1,0:T(8,128)} %get-tuple-element.150) | copy-start | bytes 49156
  68.2 5.3 %copy-start.83 = (f32[32,128]{1,0:T(8,128)S(1)}, f32[32,128]{1,0:T(8,128)}, u32[]{:S(2)}) copy-start(f32[32,128]{1,0:T(8,128)} %get-tuple-element.176) | copy-start | bytes 49156
  68.2 5.3 %copy-start.85 = (f32[32,128]{1,0:T(8,128)S(1)}, f32[32,128]{1,0:T(8,128)}, u32[]{:S(2)}) copy-start(f32[32,128]{1,0:T(8,128)} %get-tuple-element.177) | copy-start | bytes 49156
  68.2 5.3 %copy-start.87 = (f32[32,128]{1,0:T(8,128)S(1)}, f32[32,128]{1,0:T(8,128)}, u32[]{:S(2)}) copy-start(f32[32,128]{1,0:T(8,128)} %get-tuple-element.178) | copy-start | bytes 49156
  76.4 20.8 %copy-start.89 = (f32[4,32,2,128]{3,2,1,0:T(2,128)}, f32[4,32,2,128]{3,2,1,0:T(2,128)S(1)}, u32[]{:S(2)}) copy-start(f32[4,32,2,128]{3,2,1,0:T(2,128)S(1)} %get-tuple-element.119) | copy-start | bytes 393220
  76.4 1.3 collective-permute-start.11
  77.8 5.6 %collective-permute-start.12 = (f32[4,32,2,128]{3,2,1,0:T(2,128)S(1)}, f32[4,32,2,128]{3,2,1,0:T(2,128)S(1)}, u32[]{:S(2)}, u32[]{:S(2)}) collective-permute-start(f32[4,32,2,128]{3,2,1,0:T(2,128)S(1)} %collective-permute-done.11), channel_id=1, source_target_pairs={{0,16},{8,24},{16,0},{24,8},{32,48},{40,56},{48,32},{56,40},{64,80... | collective-permute-start | bytes 393224 | tf_op jit(solution)/shard_map/ppermute | solution.py:18
  83.3 8.5 %collective-permute-start.13 = (f32[4,32,2,128]{3,2,1,0:T(2,128)S(1)}, f32[4,32,2,128]{3,2,1,0:T(2,128)}, u32[]{:S(2)}, u32[]{:S(2)}) collective-permute-start(f32[4,32,2,128]{3,2,1,0:T(2,128)S(1)} %collective-permute-done.12), channel_id=1, source_target_pairs={{0,32},{8,40},{16,48},{24,56},{32,0},{40,8},{48,16},{56,24},{64,96... | collective-permute-start | bytes 393224 | tf_op jit(solution)/shard_map/ppermute | solution.py:18
  91.9 26.0 %collective-permute-start.14 = (f32[4,32,2,128]{3,2,1,0:T(2,128)}, f32[4,32,2,128]{3,2,1,0:T(2,128)}, u32[]{:S(2)}, u32[]{:S(2)}) collective-permute-start(f32[4,32,2,128]{3,2,1,0:T(2,128)} %collective-permute-done.13), channel_id=1, source_target_pairs={{0,64},{8,72},{16,80},{24,88},{32,96},{40,104},{48,112},{56,120},{... | collective-permute-start | bytes 393224 | tf_op jit(solution)/shard_map/ppermute | solution.py:18
  99.7 12.1 %collective-permute-start.9 = (f32[4,32,32,2]{2,1,3,0:T(8,128)S(1)}, f32[4,32,32,2]{2,1,3,0:T(8,128)}, u32[]{:S(2)}, u32[]{:S(2)}) collective-permute-start(f32[4,32,32,2]{2,1,3,0:T(8,128)S(1)} %copy.11), channel_id=1, source_target_pairs={{8,0},{16,8},{24,16},{32,24},{40,32},{48,40},{56,48},{64,56},{72,6... | collective-permute-start | bytes 98312 | tf_op jit(solution)/shard_map/ppermute | solution.py:31
  105.3 9.6 %collective-permute-start.10 = (f32[4,32,32,2]{2,1,3,0:T(8,128)}, f32[4,32,32,2]{2,1,3,0:T(8,128)}, u32[]{:S(2)}, u32[]{:S(2)}) collective-permute-start(f32[4,32,32,2]{2,1,3,0:T(8,128)} %copy.13), channel_id=1, source_target_pairs={{0,8},{8,16},{16,24},{24,32},{32,40},{40,48},{48,56},{56,64},{64,7... | collective-permute-start | bytes 98312 | tf_op jit(solution)/shard_map/ppermute | solution.py:29
  105.3 21.7 %collective-permute-start.17 = (f32[4,32,2,128]{3,2,1,0:T(2,128)}, f32[4,32,2,128]{3,2,1,0:T(2,128)S(1)}, u32[]{:S(2)}, u32[]{:S(2)}) collective-permute-start(f32[4,32,2,128]{3,2,1,0:T(2,128)} %copy-done.89), channel_id=1, source_target_pairs={{0,1},{1,2},{2,3},{3,4},{4,5},{5,6},{6,7},{8,9},{9,10},{10,11},{11... | collective-permute-start | bytes 393224 | tf_op jit(solution)/shard_map/ppermute | solution.py:29
  106.5 19.5 %collective-permute-start.16 = (f32[4,32,2,128]{3,2,1,0:T(2,128)}, f32[4,32,2,128]{3,2,1,0:T(2,128)}, u32[]{:S(2)}, u32[]{:S(2)}) collective-permute-start(f32[4,32,2,128]{3,2,1,0:T(2,128)} %get-tuple-element.118), channel_id=1, source_target_pairs={{1,0},{2,1},{3,2},{4,3},{5,4},{6,5},{7,6},{9,8},{10,9},{11,10},{12... | collective-permute-start | bytes 393224 | tf_op jit(solution)/shard_map/ppermute | solution.py:31
  117.9 6.8 %collective-permute-start.15 = (f32[4,32,2,128]{3,2,1,0:T(2,128)}, f32[4,32,2,128]{3,2,1,0:T(2,128)}, u32[]{:S(2)}, u32[]{:S(2)}) collective-permute-start(f32[4,32,2,128]{3,2,1,0:T(2,128)} %collective-permute-done.14), channel_id=1, source_target_pairs={{0,128},{8,136},{16,144},{24,152},{32,160},{40,168},{48,176},{56,1... | collective-permute-start | bytes 393224 | tf_op jit(solution)/shard_map/ppermute | solution.py:18
  130.4 5.3 %copy-start.20 = (f32[1,32,128]{2,1,0:T(8,128)S(1)}, f32[1,32,128]{2,1,0:T(8,128)}, u32[]{:S(2)}) copy-start(f32[1,32,128]{2,1,0:T(8,128)} %copy-done.18) | copy-start | bytes 49156
  130.4 5.3 %copy-start.23 = (f32[1,32,128]{2,1,0:T(8,128)S(1)}, f32[1,32,128]{2,1,0:T(8,128)}, u32[]{:S(2)}) copy-start(f32[1,32,128]{2,1,0:T(8,128)} %copy-done.21) | copy-start | bytes 49156
  130.4 5.3 %copy-start.26 = (f32[1,32,128]{2,1,0:T(8,128)S(1)}, f32[1,32,128]{2,1,0:T(8,128)}, u32[]{:S(2)}) copy-start(f32[1,32,128]{2,1,0:T(8,128)} %copy-done.24) | copy-start | bytes 49156
  130.4 5.3 %copy-start.28 = (f32[32,128]{1,0:T(8,128)S(1)}, f32[32,128]{1,0:T(8,128)}, u32[]{:S(2)}) copy-start(f32[32,128]{1,0:T(8,128)} %get-tuple-element.167) | copy-start | bytes 49156
  130.4 5.3 %copy-start.30 = (f32[32,128]{1,0:T(8,128)S(1)}, f32[32,128]{1,0:T(8,128)}, u32[]{:S(2)}) copy-start(f32[32,128]{1,0:T(8,128)} %get-tuple-element.168) | copy-start | bytes 49156
  130.4 5.3 %copy-start.32 = (f32[32,128]{1,0:T(8,128)S(1)}, f32[32,128]{1,0:T(8,128)}, u32[]{:S(2)}) copy-start(f32[32,128]{1,0:T(8,128)} %get-tuple-element.169) | copy-start | bytes 49156
  130.4 5.3 %copy-start.34 = (f32[32,128]{1,0:T(8,128)S(1)}, f32[32,128]{1,0:T(8,128)}, u32[]{:S(2)}) copy-start(f32[32,128]{1,0:T(8,128)} %get-tuple-element.170) | copy-start | bytes 49156
  130.4 5.3 %copy-start.36 = (f32[32,128]{1,0:T(8,128)S(1)}, f32[32,128]{1,0:T(8,128)}, u32[]{:S(2)}) copy-start(f32[32,128]{1,0:T(8,128)} %get-tuple-element.171) | copy-start | bytes 49156
  130.4 5.3 %copy-start.38 = (f32[32,128]{1,0:T(8,128)S(1)}, f32[32,128]{1,0:T(8,128)}, u32[]{:S(2)}) copy-start(f32[32,128]{1,0:T(8,128)} %get-tuple-element.172) | copy-start | bytes 49156
  (49 other events, 193.4 us)
where the time goes:
time: 142 us; the launch traced here: 140 us
  local copies, waits for them, and re-layouts  45.1 us (32%)
  starting transfers between devices  33.4 us (24%)
  other arithmetic  33.3 us (23%)
  waiting for transfers between devices  26.3 us (19%)
  between operations  1.97 us (1%)
    ppermute x10, waiting for transfers between devices, partner(): lax.ppermute(array, axis, [(i, i ^ 1 << distance) for i in range(lax.axis...  26.2 us
    ppermute x4, starting transfers between devices, padded(): lax.ppermute(head, axis, [((i + 1) % count, i) for i in range(ends)])  20.1 us
    slice x6, local copies, waits for them, and re-layouts, padded(): head = lax.slice_in_dim(cells, 0, width, axis=dim)  12.7 us
    ppermute x10, starting transfers between devices, partner(): lax.ppermute(array, axis, [(i, i ^ 1 << distance) for i in range(lax.axis...  10.8 us
    another operation x4, other arithmetic, pressure(): return gravity * (jnp.cumsum(density, axis=0) - 0.5 * density)  10.3 us
    unnamed x220, local copies, waits for them, and re-layouts  9.93 us
    mul x2, other arithmetic, explicit(): return (state + time_step * (lateral_mix * spread - carried + force)) * wet  9.78 us
    slice x2, local copies, waits for them, and re-layouts, padded(): lax.slice_in_dim(cells, cells.shape[dim] - width, cells.shape[dim], axis=...  6.25 us
  transfers between devices with their start and end apart: 18, of which 7 were waited for; matrix products, arithmetic and copies ran while one was open for 34% of the time, Pallas kernels for 0%

commit v1 on v0

v1 whole, which is shorter than its diff:
```python
import functools

import jax
import jax.numpy as jnp
from jax import lax
from jax.experimental import pallas as pl
from jax.experimental.pallas import tpu as pltpu
from jax.sharding import PartitionSpec as P

MESH = pl.DeviceIdType.MESH
FIELDS, LEVELS, ROWS, COLS = 4, 32, 32, 128
TOP = 8
DEPTH = 48
GROUPS = ((0,), (1,), (2,), (3,))
INNER, OUTER = (1, 2), (0, 3)
SLOT = {1: 0, 2: 1, 0: 2, 3: 3}
UNROLL = 2


def factors():
    inside, last, ratio = [], [], 0.0
    for level in range(LEVELS):
        low = 0.5 if level > 0 else 0.0
        inside.append(0.5 / (1.5 + low + low * ratio))
        last.append(0.5 / (1.0 + low + low * ratio))
        ratio = -0.5 / (1.5 + low + low * ratio)
    return inside, last


def kernel(
    lons, lats, state_ref, land_ref, depth_ref, out_ref,
    cur, pivot, mask, send_lon, recv_lon, halo, result,
    load_sem, lat_send, lat_recv, lon_send, lon_recv, out_sem,
):
    lon, lat = lax.axis_index("lon"), lax.axis_index("lat")
    west = {"lon": lax.rem(lon + lons - 1, lons)}
    east = {"lon": lax.rem(lon + 1, lons)}
    north, south = {"lat": lat + 1}, {"lat": lat - 1}
    fold = {"lon": lons - 1 - lon}
    is_top, is_bottom = lat == lats - 1, lat == 0
    not_top, not_bottom = lat < lats - 1, lat > 0

    barrier = pltpu.get_barrier_semaphore()

    def greet(device):
        pl.semaphore_signal(barrier, inc=1, device_id=device, device_id_type=MESH)

    greet(west)
    greet(east)
    pl.when(not_top)(lambda: greet(north))
    pl.when(is_top)(lambda: greet(fold))
    pl.when(not_bottom)(lambda: greet(south))

    loads = [
        pltpu.make_async_copy(land_ref, mask.at[0], load_sem.at[4]),
        pltpu.make_async_copy(depth_ref, mask.at[1], load_sem.at[5]),
    ] + [
        pltpu.make_async_copy(
            state_ref.at[f], cur.at[0, f, :, pl.ds(TOP, ROWS)], load_sem.at[f]
        )
        for f in range(FIELDS)
    ]
    for load in loads:
        load.start()

    lane = lax.broadcasted_iota(jnp.int32, (8, COLS), 1)
    sublane = lax.broadcasted_iota(jnp.int32, (8, COLS), 0)
    low_pair = lax.rem(lane, 4) < 2
    group_lane = lane // 4
    lane_0, lane_1 = lane == 0, lane <= 1
    lane_127, lane_126 = lane == COLS - 1, lane >= COLS - 2

    def coriolis(tile):
        row = (lat * ROWS + tile * 8 + sublane).astype(jnp.float32)
        return 0.2 * (0.2 + 0.8 * ((row + 0.5) / (lats * ROWS)))

    @pl.when(is_bottom)
    def _():
        def clear(i, carry):
            for step in range(2):
                for f in range(FIELDS):
                    cur[step, f, i, pl.ds(TOP - 2, 2), :] = jnp.zeros((2, COLS), jnp.float32)
            return carry

        lax.fori_loop(0, LEVELS, clear, 0)

    loads[0].wait()
    loads[1].wait()
    inside, last = factors()
    wet_count = []
    for tile in range(4):
        rows = pl.ds(8 * tile, 8)
        count = jnp.where(mask[0, rows, :] == 1, mask[1, rows, :], 0)
        wet_count.append(count)
        for level in range(LEVELS):
            pivot[level, rows, :] = jnp.where(
                count > level + 1, inside[level], jnp.where(count == level + 1, last[level], 0.0)
            )

    def lat_copies(step, index):
        group = GROUPS[index]
        fields = pl.ds(group[0], len(group))

        def rows(start):
            return cur.at[step, fields, :, pl.ds(start, 2)]

        up = (rows(TOP + ROWS - 2), rows(TOP - 2))
        down = (rows(TOP), rows(TOP + ROWS))
        to_fold = (rows(TOP + ROWS - 2), rows(TOP + ROWS))

        def remote(pair, side, sem_side, device):
            return pltpu.make_async_remote_copy(
                src_ref=pair[0],
                dst_ref=pair[1],
                send_sem=lat_send.at[step, side, index],
                recv_sem=lat_recv.at[step, sem_side, index],
                device_id=device,
                device_id_type=MESH,
            )

        return remote(up, 0, 0, north), remote(to_fold, 0, 1, fold), remote(down, 1, 1, south)

    def send_lat(step, index):
        up, across, down = lat_copies(step, index)
        pl.when(not_top)(lambda: up.start())
        pl.when(is_top)(lambda: across.start())
        pl.when(not_bottom)(lambda: down.start())

    def wait_lat(step, index):
        up, across, down = lat_copies(step, index)
        down.wait_recv()
        pl.when(not_bottom)(lambda: up.wait_recv())

        @pl.when(is_top)
        def _():
            reverse = (COLS - 1) - lax.broadcasted_iota(jnp.int32, (2, COLS), 1)

            def turn(level, carry):
                for f in GROUPS[index]:
                    got = cur[step, f, level, pl.ds(TOP + ROWS, 2), :]
                    got = jnp.take_along_axis(got, reverse, axis=1)
                    sign = 1.0 if f < 2 else -1.0
                    cur[step, f, level, pl.ds(TOP + ROWS, 1), :] = sign * got[1:2]
                    cur[step, f, level, pl.ds(TOP + ROWS + 1, 1), :] = sign * got[0:1]
                return carry

            lax.fori_loop(0, LEVELS, turn, 0)

    parts = ((pl.ds(0, 2), pl.ds(0, 2)), (pl.ds(2, 2), pl.ds(0, 1)), (pl.ds(2, 2), pl.ds(1, 1)))

    def lon_copies(step, part):
        tiles, pairs = parts[part]

        def remote(side, device):
            return pltpu.make_async_remote_copy(
                src_ref=send_lon.at[step, side, tiles, pairs],
                dst_ref=recv_lon.at[step, side, tiles, pairs],
                send_sem=lon_send.at[step, side, part],
                recv_sem=lon_recv.at[step, side, part],
                device_id=device,
                device_id_type=MESH,
            )

        return remote(0, east), remote(1, west)

    def pack_lon(step, tile, pair, first, second):
        slot = SLOT[tile]
        send_lon[step, 0, slot, pair] = jnp.where(low_pair, first, pltpu.roll(second, 2, 1))
        send_lon[step, 1, slot, pair] = jnp.where(low_pair, pltpu.roll(first, COLS - 2, 1), second)

    def send_lon_part(step, part):
        for copy in lon_copies(step, part):
            copy.start()

    def wait_lon(step, part):
        for copy in lon_copies(step, part):
            copy.wait_recv()
        tiles = INNER if part == 0 else OUTER
        pairs = (0, 1) if part == 0 else (part - 1,)
        for tile in tiles:
            for pair in pairs:
                from_west = recv_lon[step, 0, SLOT[tile], pair]
                from_east = recv_lon[step, 1, SLOT[tile], pair]
                halo[2 * pair, tile] = jnp.where(low_pair, from_west, pltpu.roll(from_east, 2, 1))
                halo[2 * pair + 1, tile] = jnp.where(
                    low_pair, pltpu.roll(from_west, COLS - 2, 1), from_east
                )

    def collect(level, value, packed):
        return jnp.where(group_lane == level, pltpu.roll(value, 4 * level + 2, 1), packed)

    zero = jnp.zeros((8, COLS), jnp.float32)

    for load in loads[2:]:
        load.wait()
    first_packs = {}
    for tiles in (OUTER, INNER):
        def cover(level, packs):
            packs = list(packs)
            at = 0
            for tile in tiles:
                wet = wet_count[tile] > level
                for f in range(FIELDS):
                    rows = pl.ds(TOP + 8 * tile, 8)
                    value = jnp.where(wet, cur[0, f, level, rows, :], 0.0)
                    cur[0, f, level, rows, :] = value
                    packs[at] = collect(level, value, packs[at])
                    at += 1
            return tuple(packs)

        packs = lax.fori_loop(0, LEVELS, cover, (zero,) * (4 * len(tiles)))
        for i, tile in enumerate(tiles):
            for pair in range(2):
                pack_lon(0, tile, pair, packs[4 * i + 2 * pair], packs[4 * i + 2 * pair + 1])
        if tiles == OUTER:
            pl.when(is_bottom)(lambda: pl.semaphore_wait(barrier, 3))
            pl.when(not_bottom)(lambda: pl.semaphore_wait(barrier, 4))
            for index in range(len(GROUPS)):
                send_lat(0, index)
    for part in range(3):
        send_lon_part(0, part)

    def advance(step, tiles, fields):
        force_x, force_y = 2 in fields, 3 in fields
        coriolis_of = {tile: coriolis(tile) for tile in tiles}
        units = [(tile, f) for tile in tiles for f in fields]
        forces = [(tile, axis) for tile in tiles for axis, on in enumerate((force_x, force_y)) if on]

        def store(f, level, tile, value):
            if step == 0:
                cur[1, f, level, pl.ds(TOP + 8 * tile, 8), :] = value
            else:
                result[f, level, pl.ds(8 * tile, 8), :] = value

        def load(f, level, tile):
            if step == 0:
                return cur[1, f, level, pl.ds(TOP + 8 * tile, 8), :]
            return result[f, level, pl.ds(8 * tile, 8), :]

        def at(f, level, tile, shift):
            return cur[step, f, level, pl.ds(TOP + 8 * tile + shift, 8), :]

        def down(level, carry):
            parts_done = dict(zip(units, carry[0]))
            sums = dict(zip(forces, carry[1]))
            for tile in tiles:
                own = {}

                def value(f):
                    if f not in own:
                        own[f] = at(f, level, tile, 0)
                    return own[f]

                edges = {}

                def edge(f):
                    if f not in edges:
                        edges[f] = pltpu.roll(halo[f, tile], 126 - 4 * level, 1)
                    return edges[f]

                near = {}

                def beside(f):
                    if (f, 0) not in near:
                        near[f, 0] = (
                            pltpu.roll(jnp.where(lane_0, edge(f), value(f)), COLS - 1, 1),
                            pltpu.roll(jnp.where(lane_127, edge(f), value(f)), 1, 1),
                        )
                    return near[f, 0]

                def above(f):
                    if (f, 1) not in near:
                        near[f, 1] = (at(f, level, tile, 1), at(f, level, tile, -1))
                    return near[f, 1]

                speed_x = value(2) * (1.0 / 60.0)
                speed_y = value(3) * (1.0 / 60.0)
                speed_x8, speed_y8 = 8.0 * speed_x, 8.0 * speed_y
                to_east, to_west = 0.1 - speed_x8, 0.1 + speed_x8
                to_north, to_south = 0.1 - speed_y8, 0.1 + speed_y8
                pivots = pivot[level, pl.ds(8 * tile, 8), :]
                for f in fields:
                    east_1, west_1 = beside(f)
                    east_2 = pltpu.roll(jnp.where(lane_1, edge(f), value(f)), COLS - 2, 1)
                    west_2 = pltpu.roll(jnp.where(lane_126, edge(f), value(f)), 2, 1)
                    north_1, south_1 = above(f)
                    north_2, south_2 = at(f, level, tile, 2), at(f, level, tile, -2)
                    total = (
                        (1.6 * value(f) + (east_1 * to_east + west_1 * to_west))
                        + (east_2 - west_2) * speed_x
                    ) + (
                        (north_1 * to_north + south_1 * to_south)
                        + (north_2 - south_2) * speed_y
                    )
                    if f >= 2:
                        sides = beside if f == 2 else above
                        plus_t, minus_t = sides(0)
                        plus_s, minus_s = sides(1)
                        half = 0.02 * (plus_s - minus_s) - 0.005 * (plus_t - minus_t)
                        middle = sums[tile, f - 2] + half
                        sums[tile, f - 2] = middle + half
                        turned = coriolis_of[tile] * value(5 - f)
                        total = total + ((turned if f == 2 else -turned) - middle)
                    part = pivots * (total + parts_done[tile, f])
                    parts_done[tile, f] = part
                    store(f, level, tile, part)
            return tuple(parts_done[u] for u in units), tuple(sums[k] for k in forces)

        def down_some(i, carry):
            for j in range(UNROLL):
                carry = down(i * UNROLL + j, carry)
            return carry

        lax.fori_loop(0, LEVELS // UNROLL, down_some, ((zero,) * len(units), (zero,) * len(forces)))

        def up(level, carry):
            values, packs = list(carry[0]), list(carry[1])
            for at_unit, (tile, f) in enumerate(units):
                pivots = pivot[level, pl.ds(8 * tile, 8), :]
                value = load(f, level, tile) + pivots * values[at_unit]
                store(f, level, tile, value)
                values[at_unit] = value
                if step == 0:
                    packs[at_unit] = collect(level, value, packs[at_unit])
            return tuple(values), tuple(packs)

        def up_some(i, carry):
            for j in range(UNROLL):
                carry = up(LEVELS - 1 - (i * UNROLL + j), carry)
            return carry

        start = ((zero,) * len(units), (zero,) * (len(units) if step == 0 else 0))
        packs = lax.fori_loop(0, LEVELS // UNROLL, up_some, start)[1]
        return dict(zip(units, packs))

    outs = []

    def write(fields, start, count):
        copy = pltpu.make_async_copy(
            result.at[fields, :, pl.ds(start, count)],
            out_ref.at[fields, :, pl.ds(start, count)],
            out_sem.at[len(outs)],
        )
        copy.start()
        outs.append(copy)

    every = tuple(range(FIELDS))
    for step in range(2):
        wait_lon(step, 0)
        packs = advance(step, INNER, every)
        if step == 0:
            for tile in INNER:
                for pair in range(2):
                    pack_lon(1, tile, pair, packs[tile, 2 * pair], packs[tile, 2 * pair + 1])
            send_lon_part(1, 0)
        else:
            write(pl.ds(0, FIELDS), 8, 16)
        wait_lon(step, 1)
        wait_lon(step, 2)
        packs = {}
        for index, group in enumerate(GROUPS):
            wait_lat(step, index)
            packs.update(advance(step, OUTER, group))
            if step == 0:
                send_lat(1, index)
                for pair in range(2):
                    if group[-1] == 2 * pair + 1:
                        for tile in OUTER:
                            pack_lon(1, tile, pair, packs[tile, 2 * pair], packs[tile, 2 * pair + 1])
                        send_lon_part(1, 1 + pair)
            else:
                write(pl.ds(group[0], len(group)), 0, 8)
                write(pl.ds(group[0], len(group)), 24, 8)

    for step in range(2):
        for index in range(len(GROUPS)):
            up, across, down = lat_copies(step, index)
            up.wait_send()
            pl.when(not_bottom)(lambda: down.wait_send())
        for part in range(3):
            for copy in lon_copies(step, part):
                copy.wait_send()
    for copy in outs:
        copy.wait()


def per_device(lons, lats, state, land_mask, wet_levels):
    any_spec = pl.BlockSpec(memory_space=pl.ANY)
    groups = len(GROUPS)
    return pl.pallas_call(
        functools.partial(kernel, lons, lats),
        out_shape=jax.ShapeDtypeStruct(state.shape, jnp.float32),
        in_specs=[any_spec] * 3,
        out_specs=any_spec,
        scratch_shapes=[
            pltpu.VMEM((2, FIELDS, LEVELS, DEPTH, COLS), jnp.float32),
            pltpu.VMEM((LEVELS, ROWS, COLS), jnp.float32),
            pltpu.VMEM((2, ROWS, COLS), jnp.int32),
            pltpu.VMEM((2, 2, 4, 2, 8, COLS), jnp.float32),
            pltpu.VMEM((2, 2, 4, 2, 8, COLS), jnp.float32),
            pltpu.VMEM((FIELDS, 4, 8, COLS), jnp.float32),
            pltpu.VMEM((FIELDS, LEVELS, ROWS, COLS), jnp.float32),
            pltpu.SemaphoreType.DMA((6,)),
            pltpu.SemaphoreType.DMA((2, 2, groups)),
            pltpu.SemaphoreType.DMA((2, 2, groups)),
            pltpu.SemaphoreType.DMA((2, 2, 3)),
            pltpu.SemaphoreType.DMA((2, 2, 3)),
            pltpu.SemaphoreType.DMA((1 + 2 * groups,)),
        ],
        compiler_params=pltpu.CompilerParams(collective_id=0, has_side_effects=True),
        name="ocean_steps",
    )(state, land_mask, wet_levels)


def solution(mesh):
    placed = (P(None, None, "lat", "lon"), P("lat", "lon"), P("lat", "lon"))
    return jax.shard_map(
        functools.partial(per_device, mesh.shape["lon"], mesh.shape["lat"]),
        mesh=mesh,
        in_specs=placed,
        out_specs=P(None, None, "lat", "lon"),
        check_vma=False,
    )
```

time: 142 us -> 76 us (0.54); the launches traced: 140 us -> 75.8 us
  Pallas kernels: 0 us -> 72.8 us
  local copies, waits for them, and re-layouts: 45.1 us -> 3.08 us
  starting transfers between devices: 33.4 us -> 0 us
  other arithmetic: 33.3 us -> 0 us
  waiting for transfers between devices: 26.3 us -> 0 us
  between operations: 1.97 us -> 0.01 us
    pallas_call x0 -> x1, Pallas kernels: none -> 72.8 us  [per_device(): pl.pallas_call(functools.partial(kernel, lons, lats), out_shape=jax.Shape...]
    ppermute x18 -> x0, starting transfers between devices: 33.4 us -> none  [the longest x4 20.1 us: padded(): lax.ppermute(head, axis, [((i + 1) % count, i) for i in range(ends)])]
    ppermute x18 -> x0, waiting for transfers between devices: 26.3 us -> none  [the longest x10 26.2 us: partner(): lax.ppermute(array, axis, [(i, i ^ 1 << distance) for i in range(lax.axis...]
    slice x8 -> x0, local copies, waits for them, and re-layouts: 19 us -> none  [the longest x6 12.7 us: padded(): head = lax.slice_in_dim(cells, 0, width, axis=dim)]
    mul x22 -> x0, other arithmetic: 14.3 us -> none  [the longest x2 9.78 us: explicit(): return (state + time_step * (lateral_mix * spread - carried + force)) * wet]
    ppermute x4 -> x0, local copies, waits for them, and re-layouts: 12.2 us -> none  [the longest x2 6.09 us: padded(): lax.ppermute(tail, axis, [(i, (i + 1) % count) for i in range(ends)])]
    another operation x6 -> x0, other arithmetic: 11 us -> none  [the longest x4 10.3 us: pressure(): return gravity * (jnp.cumsum(density, axis=0) - 0.5 * density)]
    unnamed x220 -> x1, local copies, waits for them, and re-layouts: 9.93 us -> 3.08 us
  transfers between devices with their start and end apart: 18 -> 0, of which waited for: 7 -> 0; matrix products, arithmetic and copies ran while one was open for 34% -> 0% of each run, Pallas kernels for 0% -> 0%
where the time goes in v1:
time: 76 us; the launch traced here: 75.8 us
  Pallas kernels  72.8 us (96%)
  local copies, waits for them, and re-layouts  3.08 us (4%)
    pallas_call x1, Pallas kernels, per_device(): pl.pallas_call(functools.partial(kernel, lons, lats), out_shape=jax.Shape...  72.8 us
    unnamed x1, local copies, waits for them, and re-layouts  3.08 us

profile of v1, /device:TPU:14, one launch (start us, length us, event | category | flops | bytes accessed | tf_op | source)
XLA Modules:
  0.0 75.8 jit_solution(12417257767716513849)
XLA Ops:
  0.0 72.8 %ocean_steps.1 = f32[4,32,32,128]{3,2,1,0:T(8,128)} custom-call(f32[4,32,32,128]{3,2,1,0:T(8,128)} %state_ref.1, s32[32,128]{1,0:T(8,128)} %land_ref.1, s32[32,128]{1,0:T(8,128)} %depth_ref.1), custom_call_target="tpu_custom_call" | custom-call | tf_op jit(solution)/shard_map/ocean_steps/pallas_call | solution.py:390
  72.8 3.1 %copy.5 = f32[4,32,32,128]{3,2,1,0:T(8,128)} copy(f32[4,32,32,128]{3,2,1,0:T(8,128)} %ocean_steps.1) | data formatting | bytes 4194304

commit v2 on v1

--- a/solution.py
+++ b/solution.py
@@ -14,7 +14,12 @@
 GROUPS = ((0,), (1,), (2,), (3,))
 INNER, OUTER = (1, 2), (0, 3)
 SLOT = {1: 0, 2: 1, 0: 2, 3: 3}
-UNROLL = 2
+COVER = 8
+X_UNROLL, Y_UNROLL = 4, 8
+
+
+def repeat(count, body, carry):
+    return body(0, carry) if count == 1 else lax.fori_loop(0, count, body, carry)
 
 
 def factors():
@@ -29,7 +34,7 @@
 
 def kernel(
     lons, lats, state_ref, land_ref, depth_ref, out_ref,
-    cur, pivot, mask, send_lon, recv_lon, halo, result,
+    cur, pivot, mask, send_lon, recv_lon, halo, edges, result,
     load_sem, lat_send, lat_recv, lon_send, lon_recv, out_sem,
 ):
     lon, lat = lax.axis_index("lon"), lax.axis_index("lat")
@@ -135,16 +140,13 @@
         def _():
             reverse = (COLS - 1) - lax.broadcasted_iota(jnp.int32, (2, COLS), 1)
 
-            def turn(level, carry):
+            for level in range(LEVELS):
                 for f in GROUPS[index]:
                     got = cur[step, f, level, pl.ds(TOP + ROWS, 2), :]
                     got = jnp.take_along_axis(got, reverse, axis=1)
                     sign = 1.0 if f < 2 else -1.0
                     cur[step, f, level, pl.ds(TOP + ROWS, 1), :] = sign * got[1:2]
                     cur[step, f, level, pl.ds(TOP + ROWS + 1, 1), :] = sign * got[0:1]
-                return carry
-
-            lax.fori_loop(0, LEVELS, turn, 0)
 
     parts = ((pl.ds(0, 2), pl.ds(0, 2)), (pl.ds(2, 2), pl.ds(0, 1)), (pl.ds(2, 2), pl.ds(1, 1)))
 
@@ -186,8 +188,12 @@
                     low_pair, pltpu.roll(from_west, COLS - 2, 1), from_east
                 )
 
-    def collect(level, value, packed):
-        return jnp.where(group_lane == level, pltpu.roll(value, 4 * level + 2, 1), packed)
+    def collect(place, value, packed):
+        return jnp.where(group_lane == place, pltpu.roll(value, 4 * place + 2, 1), packed)
+
+    def turn_lanes(value, amount):
+        amount = amount % COLS
+        return value if amount == 0 else pltpu.roll(value, amount, 1)
 
     zero = jnp.zeros((8, COLS), jnp.float32)
 
@@ -195,20 +201,22 @@
         load.wait()
     first_packs = {}
     for tiles in (OUTER, INNER):
-        def cover(level, packs):
+        def cover(i, packs):
             packs = list(packs)
-            at = 0
-            for tile in tiles:
-                wet = wet_count[tile] > level
-                for f in range(FIELDS):
-                    rows = pl.ds(TOP + 8 * tile, 8)
-                    value = jnp.where(wet, cur[0, f, level, rows, :], 0.0)
-                    cur[0, f, level, rows, :] = value
-                    packs[at] = collect(level, value, packs[at])
-                    at += 1
-            return tuple(packs)
-
-        packs = lax.fori_loop(0, LEVELS, cover, (zero,) * (4 * len(tiles)))
+            for place in range(COVER):
+                level = i * COVER + place
+                at = 0
+                for tile in tiles:
+                    wet = wet_count[tile] > level
+                    for f in range(FIELDS):
+                        rows = pl.ds(TOP + 8 * tile, 8)
+                        value = jnp.where(wet, cur[0, f, level, rows, :], 0.0)
+                        cur[0, f, level, rows, :] = value
+                        packs[at] = collect(place, value, packs[at])
+                        at += 1
+            return tuple(turn_lanes(pack, -4 * COVER) for pack in packs)
+
+        packs = repeat(LEVELS // COVER, cover, (zero,) * (4 * len(tiles)))
         for i, tile in enumerate(tiles):
             for pair in range(2):
                 pack_lon(0, tile, pair, packs[4 * i + 2 * pair], packs[4 * i + 2 * pair + 1])
@@ -220,118 +228,115 @@
     for part in range(3):
         send_lon_part(0, part)
 
-    def advance(step, tiles, fields):
-        force_x, force_y = 2 in fields, 3 in fields
-        coriolis_of = {tile: coriolis(tile) for tile in tiles}
+    def grow(step, f, level, tile):
+        if step == 0:
+            return cur.at[1, f, level, pl.ds(TOP + 8 * tile, 8), :]
+        return result.at[f, level, pl.ds(8 * tile, 8), :]
+
+    def at(step, f, level, tile, shift=0):
+        return cur[step, f, level, pl.ds(TOP + 8 * tile + shift, 8), :]
+
+    def spread_edges(tiles, fields):
+        for tile in tiles:
+            for f in fields:
+                packed = halo[f, tile]
+                for level in range(LEVELS):
+                    edges[f, level, pl.ds(8 * tile, 8), :] = turn_lanes(packed, 126 - 4 * level)
+
+    def sweep(step, tiles, fields, axis, last, unroll):
         units = [(tile, f) for tile in tiles for f in fields]
-        forces = [(tile, axis) for tile in tiles for axis, on in enumerate((force_x, force_y)) if on]
-
-        def store(f, level, tile, value):
-            if step == 0:
-                cur[1, f, level, pl.ds(TOP + 8 * tile, 8), :] = value
-            else:
-                result[f, level, pl.ds(8 * tile, 8), :] = value
-
-        def load(f, level, tile):
-            if step == 0:
-                return cur[1, f, level, pl.ds(TOP + 8 * tile, 8), :]
-            return result[f, level, pl.ds(8 * tile, 8), :]
-
-        def at(f, level, tile, shift):
-            return cur[step, f, level, pl.ds(TOP + 8 * tile + shift, 8), :]
-
-        def down(level, carry):
-            parts_done = dict(zip(units, carry[0]))
-            sums = dict(zip(forces, carry[1]))
+        forces = [tile for tile in tiles if 2 + axis in fields]
+        turned = {tile: coriolis(tile) for tile in tiles} if axis == 0 else None
+
+        def one(level, parts_done, sums):
             for tile in tiles:
-                own = {}
+                near = {}
 
                 def value(f):
-                    if f not in own:
-                        own[f] = at(f, level, tile, 0)
-                    return own[f]
-
-                edges = {}
+                    if (f, 0) not in near:
+                        near[f, 0] = at(step, f, level, tile)
+                    return near[f, 0]
 
                 def edge(f):
-                    if f not in edges:
-                        edges[f] = pltpu.roll(halo[f, tile], 126 - 4 * level, 1)
-                    return edges[f]
-
-                near = {}
-
-                def beside(f):
-                    if (f, 0) not in near:
-                        near[f, 0] = (
-                            pltpu.roll(jnp.where(lane_0, edge(f), value(f)), COLS - 1, 1),
-                            pltpu.roll(jnp.where(lane_127, edge(f), value(f)), 1, 1),
+                    if (f, 1) not in near:
+                        near[f, 1] = edges[f, level, pl.ds(8 * tile, 8), :]
+                    return near[f, 1]
+
+                def sides(f):
+                    if (f, 2) not in near:
+                        if axis == 0:
+                            near[f, 2] = (
+                                pltpu.roll(jnp.where(lane_0, edge(f), value(f)), COLS - 1, 1),
+                                pltpu.roll(jnp.where(lane_127, edge(f), value(f)), 1, 1),
+                            )
+                        else:
+                            near[f, 2] = at(step, f, level, tile, 1), at(step, f, level, tile, -1)
+                    return near[f, 2]
+
+                def far_sides(f):
+                    if axis == 0:
+                        return (
+                            pltpu.roll(jnp.where(lane_1, edge(f), value(f)), COLS - 2, 1),
+                            pltpu.roll(jnp.where(lane_126, edge(f), value(f)), 2, 1),
                         )
-                    return near[f, 0]
-
-                def above(f):
-                    if (f, 1) not in near:
-                        near[f, 1] = (at(f, level, tile, 1), at(f, level, tile, -1))
-                    return near[f, 1]
-
-                speed_x = value(2) * (1.0 / 60.0)
-                speed_y = value(3) * (1.0 / 60.0)
-                speed_x8, speed_y8 = 8.0 * speed_x, 8.0 * speed_y
-                to_east, to_west = 0.1 - speed_x8, 0.1 + speed_x8
-                to_north, to_south = 0.1 - speed_y8, 0.1 + speed_y8
-                pivots = pivot[level, pl.ds(8 * tile, 8), :]
+                    return at(step, f, level, tile, 2), at(step, f, level, tile, -2)
+
+                speed = value(2 + axis) * (1.0 / 60.0)
+                speed_8 = 8.0 * speed
+                to_plus, to_minus = 0.1 - speed_8, 0.1 + speed_8
                 for f in fields:
-                    east_1, west_1 = beside(f)
-                    east_2 = pltpu.roll(jnp.where(lane_1, edge(f), value(f)), COLS - 2, 1)
-                    west_2 = pltpu.roll(jnp.where(lane_126, edge(f), value(f)), 2, 1)
-                    north_1, south_1 = above(f)
-                    north_2, south_2 = at(f, level, tile, 2), at(f, level, tile, -2)
-                    total = (
-                        (1.6 * value(f) + (east_1 * to_east + west_1 * to_west))
-                        + (east_2 - west_2) * speed_x
-                    ) + (
-                        (north_1 * to_north + south_1 * to_south)
-                        + (north_2 - south_2) * speed_y
-                    )
-                    if f >= 2:
-                        sides = beside if f == 2 else above
+                    plus, minus = sides(f)
+                    plus_2, minus_2 = far_sides(f)
+                    total = (plus * to_plus + minus * to_minus) + (plus_2 - minus_2) * speed
+                    if axis == 0:
+                        total = total + 1.6 * value(f)
+                        if f == 2:
+                            total = total + turned[tile] * value(3)
+                        if f == 3:
+                            total = total - turned[tile] * value(2)
+                    if f == 2 + axis:
                         plus_t, minus_t = sides(0)
                         plus_s, minus_s = sides(1)
                         half = 0.02 * (plus_s - minus_s) - 0.005 * (plus_t - minus_t)
-                        middle = sums[tile, f - 2] + half
-                        sums[tile, f - 2] = middle + half
-                        turned = coriolis_of[tile] * value(5 - f)
-                        total = total + ((turned if f == 2 else -turned) - middle)
-                    part = pivots * (total + parts_done[tile, f])
-                    parts_done[tile, f] = part
-                    store(f, level, tile, part)
-            return tuple(parts_done[u] for u in units), tuple(sums[k] for k in forces)
-
-        def down_some(i, carry):
-            for j in range(UNROLL):
-                carry = down(i * UNROLL + j, carry)
-            return carry
-
-        lax.fori_loop(0, LEVELS // UNROLL, down_some, ((zero,) * len(units), (zero,) * len(forces)))
-
-        def up(level, carry):
-            values, packs = list(carry[0]), list(carry[1])
-            for at_unit, (tile, f) in enumerate(units):
-                pivots = pivot[level, pl.ds(8 * tile, 8), :]
-                value = load(f, level, tile) + pivots * values[at_unit]
-                store(f, level, tile, value)
-                values[at_unit] = value
-                if step == 0:
-                    packs[at_unit] = collect(level, value, packs[at_unit])
+                        middle = sums[tile] + half
+                        sums[tile] = middle + half
+                        total = total - middle
+                    ref = grow(step, f, level, tile)
+                    if last:
+                        pivots = pivot[level, pl.ds(8 * tile, 8), :]
+                        total = pivots * ((total + ref[...]) + parts_done[tile, f])
+                        parts_done[tile, f] = total
+                    ref[...] = total
+
+        def some(i, carry):
+            parts_done = dict(zip(units, carry[0]))
+            sums = dict(zip(forces, carry[1]))
+            for place in range(unroll):
+                one(i * unroll + place, parts_done, sums)
+            return tuple(parts_done[u] for u in units) if last else (), tuple(sums[k] for k in forces)
+
+        start = ((zero,) * len(units) if last else (), (zero,) * len(forces))
+        repeat(LEVELS // unroll, some, start)
+
+    def substitute(step, tiles, fields, unroll):
+        units = [(tile, f) for tile in tiles for f in fields]
+        trips = LEVELS // unroll
+
+        def some(i, carry):
+            values, packs = list(carry[0]), [turn_lanes(pack, 4 * unroll) for pack in carry[1]]
+            for place in reversed(range(unroll)):
+                level = (trips - 1 - i) * unroll + place
+                for at_unit, (tile, f) in enumerate(units):
+                    ref = grow(step, f, level, tile)
+                    value = ref[...] + pivot[level, pl.ds(8 * tile, 8), :] * values[at_unit]
+                    ref[...] = value
+                    values[at_unit] = value
+                    if step == 0:
+                        packs[at_unit] = collect(place, value, packs[at_unit])
             return tuple(values), tuple(packs)
 
-        def up_some(i, carry):
-            for j in range(UNROLL):
-                carry = up(LEVELS - 1 - (i * UNROLL + j), carry)
-            return carry
-
         start = ((zero,) * len(units), (zero,) * (len(units) if step == 0 else 0))
-        packs = lax.fori_loop(0, LEVELS // UNROLL, up_some, start)[1]
-        return dict(zip(units, packs))
+        return dict(zip(units, repeat(trips, some, start)[1]))
 
     outs = []
 
@@ -345,32 +350,49 @@
         outs.append(copy)
 
     every = tuple(range(FIELDS))
-    for step in range(2):
-        wait_lon(step, 0)
-        packs = advance(step, INNER, every)
-        if step == 0:
-            for tile in INNER:
-                for pair in range(2):
-                    pack_lon(1, tile, pair, packs[tile, 2 * pair], packs[tile, 2 * pair + 1])
-            send_lon_part(1, 0)
-        else:
-            write(pl.ds(0, FIELDS), 8, 16)
-        wait_lon(step, 1)
-        wait_lon(step, 2)
-        packs = {}
-        for index, group in enumerate(GROUPS):
-            wait_lat(step, index)
-            packs.update(advance(step, OUTER, group))
-            if step == 0:
-                send_lat(1, index)
-                for pair in range(2):
-                    if group[-1] == 2 * pair + 1:
-                        for tile in OUTER:
-                            pack_lon(1, tile, pair, packs[tile, 2 * pair], packs[tile, 2 * pair + 1])
-                        send_lon_part(1, 1 + pair)
-            else:
-                write(pl.ds(group[0], len(group)), 0, 8)
-                write(pl.ds(group[0], len(group)), 24, 8)
+
+    def pack_next(tiles, pair, packs):
+        for tile in tiles:
+            pack_lon(1, tile, pair, packs[tile, 2 * pair], packs[tile, 2 * pair + 1])
+
+    sweep(0, INNER, every, 1, False, 2)
+    for part in range(3):
+        wait_lon(0, part)
+    spread_edges(OUTER, every)
+    sweep(0, OUTER, every, 0, False, X_UNROLL)
+    spread_edges(INNER, every)
+    sweep(0, INNER, every, 0, True, X_UNROLL)
+    packs = substitute(0, INNER, every, 8)
+    for pair in range(2):
+        pack_next(INNER, pair, packs)
+    send_lon_part(1, 0)
+    packs = {}
+    for index, group in enumerate(GROUPS):
+        wait_lat(0, index)
+        sweep(0, OUTER, group, 1, True, Y_UNROLL)
+        packs.update(substitute(0, OUTER, group, 16))
+        send_lat(1, index)
+        for pair in range(2):
+            if group[-1] == 2 * pair + 1:
+                pack_next(OUTER, pair, packs)
+                send_lon_part(1, 1 + pair)
+
+    sweep(1, INNER, every, 1, False, 2)
+    wait_lon(1, 0)
+    spread_edges(INNER, every)
+    sweep(1, INNER, every, 0, True, X_UNROLL)
+    substitute(1, INNER, every, 8)
+    write(pl.ds(0, FIELDS), 8, 16)
+    for part in (1, 2):
+        wait_lon(1, part)
+    spread_edges(OUTER, every)
+    sweep(1, OUTER, every, 0, False, X_UNROLL)
+    for index, group in enumerate(GROUPS):
+        wait_lat(1, index)
+        sweep(1, OUTER, group, 1, True, Y_UNROLL)
+        substitute(1, OUTER, group, 16)
+        write(pl.ds(group[0], len(group)), 0, 8)
+        write(pl.ds(group[0], len(group)), 24, 8)
 
     for step in range(2):
         for index in range(len(GROUPS)):
@@ -400,6 +422,7 @@
             pltpu.VMEM((2, 2, 4, 2, 8, COLS), jnp.float32),
             pltpu.VMEM((FIELDS, 4, 8, COLS), jnp.float32),
             pltpu.VMEM((FIELDS, LEVELS, ROWS, COLS), jnp.float32),
+            pltpu.VMEM((FIELDS, LEVELS, ROWS, COLS), jnp.float32),
             pltpu.SemaphoreType.DMA((6,)),
             pltpu.SemaphoreType.DMA((2, 2, groups)),
             pltpu.SemaphoreType.DMA((2, 2, groups)),

time: 76 us -> 36.3 us (0.48)
  Pallas kernels: 72.8 us -> 33 us
    pallas_call x1, Pallas kernels: 72.8 us -> 33 us  [per_device(): pl.pallas_call(functools.partial(kernel, lons, lats), out_shape=jax.Shape...]
where the time goes in v2:
time: 36.3 us; the launch traced here: 36.1 us
  Pallas kernels  33 us (91%)
  local copies, waits for them, and re-layouts  3.08 us (8%)
    pallas_call x1, Pallas kernels, per_device(): pl.pallas_call(functools.partial(kernel, lons, lats), out_shape=jax.Shape...  33 us
    unnamed x1, local copies, waits for them, and re-layouts  3.08 us

profile of v2, /device:TPU:14, one launch (start us, length us, event | category | flops | bytes accessed | tf_op | source)
XLA Modules:
  0.0 36.1 jit_solution(6173153122650510992)
XLA Ops:
  0.0 33.0 %ocean_steps.1 = f32[4,32,32,128]{3,2,1,0:T(8,128)} custom-call(f32[4,32,32,128]{3,2,1,0:T(8,128)} %state_ref.1, s32[32,128]{1,0:T(8,128)} %land_ref.1, s32[32,128]{1,0:T(8,128)} %depth_ref.1), custom_call_target="tpu_custom_call" | custom-call | tf_op jit(solution)/shard_map/ocean_steps/pallas_call | solution.py:412
  33.0 3.1 %copy.5 = f32[4,32,32,128]{3,2,1,0:T(8,128)} copy(f32[4,32,32,128]{3,2,1,0:T(8,128)} %ocean_steps.1) | data formatting | bytes 4194304

commit v3 on v2

--- a/solution.py
+++ b/solution.py
@@ -33,9 +33,9 @@
 
 
 def kernel(
-    lons, lats, state_ref, land_ref, depth_ref, out_ref,
-    cur, pivot, mask, send_lon, recv_lon, halo, edges, result,
-    load_sem, lat_send, lat_recv, lon_send, lon_recv, out_sem,
+    lons, lats, state_ref, land_ref, depth_ref, result,
+    cur, pivot, mask, send_lon, recv_lon, halo, edges,
+    load_sem, lat_send, lat_recv, lon_send, lon_recv,
 ):
     lon, lat = lax.axis_index("lon"), lax.axis_index("lat")
     west = {"lon": lax.rem(lon + lons - 1, lons)}
@@ -338,17 +338,6 @@
         start = ((zero,) * len(units), (zero,) * (len(units) if step == 0 else 0))
         return dict(zip(units, repeat(trips, some, start)[1]))
 
-    outs = []
-
-    def write(fields, start, count):
-        copy = pltpu.make_async_copy(
-            result.at[fields, :, pl.ds(start, count)],
-            out_ref.at[fields, :, pl.ds(start, count)],
-            out_sem.at[len(outs)],
-        )
-        copy.start()
-        outs.append(copy)
-
     every = tuple(range(FIELDS))
 
     def pack_next(tiles, pair, packs):
@@ -382,7 +371,6 @@
     spread_edges(INNER, every)
     sweep(1, INNER, every, 0, True, X_UNROLL)
     substitute(1, INNER, every, 8)
-    write(pl.ds(0, FIELDS), 8, 16)
     for part in (1, 2):
         wait_lon(1, part)
     spread_edges(OUTER, every)
@@ -391,8 +379,6 @@
         wait_lat(1, index)
         sweep(1, OUTER, group, 1, True, Y_UNROLL)
         substitute(1, OUTER, group, 16)
-        write(pl.ds(group[0], len(group)), 0, 8)
-        write(pl.ds(group[0], len(group)), 24, 8)
 
     for step in range(2):
         for index in range(len(GROUPS)):
@@ -402,8 +388,6 @@
         for part in range(3):
             for copy in lon_copies(step, part):
                 copy.wait_send()
-    for copy in outs:
-        copy.wait()
 
 
 def per_device(lons, lats, state, land_mask, wet_levels):
@@ -412,8 +396,8 @@
     return pl.pallas_call(
         functools.partial(kernel, lons, lats),
         out_shape=jax.ShapeDtypeStruct(state.shape, jnp.float32),
-        in_specs=[any_spec] * 3,
-        out_specs=any_spec,
+        in_specs=[pl.BlockSpec(memory_space=pltpu.HBM)] * 3,
+        out_specs=pl.BlockSpec(memory_space=pltpu.VMEM),
         scratch_shapes=[
             pltpu.VMEM((2, FIELDS, LEVELS, DEPTH, COLS), jnp.float32),
             pltpu.VMEM((LEVELS, ROWS, COLS), jnp.float32),
@@ -422,17 +406,15 @@
             pltpu.VMEM((2, 2, 4, 2, 8, COLS), jnp.float32),
             pltpu.VMEM((FIELDS, 4, 8, COLS), jnp.float32),
             pltpu.VMEM((FIELDS, LEVELS, ROWS, COLS), jnp.float32),
-            pltpu.VMEM((FIELDS, LEVELS, ROWS, COLS), jnp.float32),
             pltpu.SemaphoreType.DMA((6,)),
             pltpu.SemaphoreType.DMA((2, 2, groups)),
             pltpu.SemaphoreType.DMA((2, 2, groups)),
             pltpu.SemaphoreType.DMA((2, 2, 3)),
             pltpu.SemaphoreType.DMA((2, 2, 3)),
-            pltpu.SemaphoreType.DMA((1 + 2 * groups,)),
         ],
-        compiler_params=pltpu.CompilerParams(collective_id=0, has_side_effects=True),
+        compiler_params=pltpu.CompilerParams(collective_id=0, has_side_effects=True, vmem_limit_bytes=24 * 2**20),
         name="ocean_steps",
-    )(state, land_mask, wet_levels)
+    )(*(pltpu.with_memory_space_constraint(x, pltpu.HBM) for x in (state, land_mask, wet_levels)))
 
 
 def solution(mesh):

time: 36.3 us -> 33.7 us (0.928)
  local copies, waits for them, and re-layouts: 3.08 us -> 1.32 us
  Pallas kernels: 33 us -> 32.2 us
    unnamed x1, local copies, waits for them, and re-layouts: 3.08 us -> 1.32 us
    pallas_call x1, Pallas kernels: 33 us -> 32.2 us  [per_device(): pl.pallas_call(functools.partial(kernel, lons, lats), out_shape=jax.Shape...]
where the time goes in v3:
time: 33.7 us; the launch traced here: 33.5 us
  Pallas kernels  32.2 us (96%)
  local copies, waits for them, and re-layouts  1.32 us (4%)
    pallas_call x1, Pallas kernels, per_device(): pl.pallas_call(functools.partial(kernel, lons, lats), out_shape=jax.Shape...  32.2 us
    unnamed x1, local copies, waits for them, and re-layouts  1.32 us

profile of v3, /device:TPU:14, one launch (start us, length us, event | category | flops | bytes accessed | tf_op | source)
XLA Modules:
  0.0 33.5 jit_solution(11705216090550567848)
XLA Ops:
  0.0 32.2 %ocean_steps.1 = f32[4,32,32,128]{3,2,1,0:T(8,128)S(1)} custom-call(f32[4,32,32,128]{3,2,1,0:T(8,128)} %state_ref.1, s32[32,128]{1,0:T(8,128)} %land_ref.1, s32[32,128]{1,0:T(8,128)} %depth_ref.1), custom_call_target="tpu_custom_call" | custom-call | tf_op jit(solution)/shard_map/ocean_steps/pallas_call | solution.py:396
  32.2 1.3 %copy.5 = f32[4,32,32,128]{3,2,1,0:T(8,128)} copy(f32[4,32,32,128]{3,2,1,0:T(8,128)S(1)} %ocean_steps.1) | data formatting | bytes 4194304

commit v4 on v3

--- a/solution.py
+++ b/solution.py
@@ -15,7 +15,7 @@
 INNER, OUTER = (1, 2), (0, 3)
 SLOT = {1: 0, 2: 1, 0: 2, 3: 3}
 COVER = 8
-X_UNROLL, Y_UNROLL = 4, 8
+X_LEVELS, Y_UNROLL = 32, 8
 
 
 def repeat(count, body, carry):
@@ -34,16 +34,18 @@
 
 def kernel(
     lons, lats, state_ref, land_ref, depth_ref, result,
-    cur, pivot, mask, send_lon, recv_lon, halo, edges,
+    cur, pivot, mask, send_lon, recv_lon, halo, edges, relayed, own, filters,
     load_sem, lat_send, lat_recv, lon_send, lon_recv,
 ):
     lon, lat = lax.axis_index("lon"), lax.axis_index("lat")
     west = {"lon": lax.rem(lon + lons - 1, lons)}
     east = {"lon": lax.rem(lon + 1, lons)}
     north, south = {"lat": lat + 1}, {"lat": lat - 1}
-    fold = {"lon": lons - 1 - lon}
+    relay = {"lon": lons - 1 - lon, "lat": lat - 1}
+    origin = {"lon": lons - 1 - lon, "lat": lat + 1}
     is_top, is_bottom = lat == lats - 1, lat == 0
     not_top, not_bottom = lat < lats - 1, lat > 0
+    is_relay = lat == lats - 2
 
     barrier = pltpu.get_barrier_semaphore()
 
@@ -53,7 +55,8 @@
     greet(west)
     greet(east)
     pl.when(not_top)(lambda: greet(north))
-    pl.when(is_top)(lambda: greet(fold))
+    pl.when(is_top)(lambda: greet(relay))
+    pl.when(is_relay)(lambda: greet(origin))
     pl.when(not_bottom)(lambda: greet(south))
 
     loads = [
@@ -70,10 +73,22 @@
 
     lane = lax.broadcasted_iota(jnp.int32, (8, COLS), 1)
     sublane = lax.broadcasted_iota(jnp.int32, (8, COLS), 0)
-    low_pair = lax.rem(lane, 4) < 2
+    quarter = lax.rem(lane, 4)
+    low_pair = quarter < 2
     group_lane = lane // 4
-    lane_0, lane_1 = lane == 0, lane <= 1
-    lane_127, lane_126 = lane == COLS - 1, lane >= COLS - 2
+
+    source = lax.broadcasted_iota(jnp.int32, (COLS, COLS), 0)
+    offset = lax.rem(source - lax.broadcasted_iota(jnp.int32, (COLS, COLS), 1) + COLS, COLS)
+
+    def weigh(plus, minus, plus_2, minus_2):
+        weights = jnp.where(offset == 1, plus, jnp.where(offset == COLS - 1, minus, 0.0))
+        weights = jnp.where(offset == 2, plus_2, jnp.where(offset == COLS - 2, minus_2, weights))
+        return weights.astype(jnp.bfloat16)
+
+    for at_filter, taps in enumerate(((1.0, 1.0, 0.0, 0.0), (8.0, -8.0, -1.0, 1.0), (1.0, -1.0, 0.0, 0.0))):
+        weights = weigh(*taps)
+        for half in range(2):
+            filters[pl.ds(COLS * half, COLS), pl.ds(COLS * at_filter, COLS)] = weights
 
     def coriolis(tile):
         row = (lat * ROWS + tile * 8 + sublane).astype(jnp.float32)
@@ -111,28 +126,43 @@
 
         up = (rows(TOP + ROWS - 2), rows(TOP - 2))
         down = (rows(TOP), rows(TOP + ROWS))
-        to_fold = (rows(TOP + ROWS - 2), rows(TOP + ROWS))
-
-        def remote(pair, side, sem_side, device):
+        held = relayed.at[step, fields, :, pl.ds(0, 2)]
+        across = (rows(TOP + ROWS - 2), held)
+        onward = (held, rows(TOP + ROWS))
+
+        def remote(pair, send_sem, recv_sem, device):
             return pltpu.make_async_remote_copy(
                 src_ref=pair[0],
                 dst_ref=pair[1],
-                send_sem=lat_send.at[step, side, index],
-                recv_sem=lat_recv.at[step, sem_side, index],
+                send_sem=send_sem.at[step, index],
+                recv_sem=recv_sem.at[step, index],
                 device_id=device,
                 device_id_type=MESH,
             )
 
-        return remote(up, 0, 0, north), remote(to_fold, 0, 1, fold), remote(down, 1, 1, south)
+        return (
+            remote(up, lat_send.at[0], lat_recv.at[0], north),
+            remote(across, lat_send.at[0], lat_recv.at[2], relay),
+            remote(down, lat_send.at[1], lat_recv.at[1], south),
+            remote(onward, lat_send.at[2], lat_recv.at[1], north),
+        )
 
     def send_lat(step, index):
-        up, across, down = lat_copies(step, index)
+        up, across, down, _ = lat_copies(step, index)
         pl.when(not_top)(lambda: up.start())
         pl.when(is_top)(lambda: across.start())
         pl.when(not_bottom)(lambda: down.start())
 
+    def hand_on(step, index):
+        _, across, _, onward = lat_copies(step, index)
+
+        @pl.when(is_relay)
+        def _():
+            across.wait_recv()
+            onward.start()
+
     def wait_lat(step, index):
-        up, across, down = lat_copies(step, index)
+        up, _, down, _ = lat_copies(step, index)
         down.wait_recv()
         pl.when(not_bottom)(lambda: up.wait_recv())
 
@@ -167,6 +197,8 @@
 
     def pack_lon(step, tile, pair, first, second):
         slot = SLOT[tile]
+        own[step, 2 * pair, tile] = first
+        own[step, 2 * pair + 1, tile] = second
         send_lon[step, 0, slot, pair] = jnp.where(low_pair, first, pltpu.roll(second, 2, 1))
         send_lon[step, 1, slot, pair] = jnp.where(low_pair, pltpu.roll(first, COLS - 2, 1), second)
 
@@ -222,7 +254,8 @@
                 pack_lon(0, tile, pair, packs[4 * i + 2 * pair], packs[4 * i + 2 * pair + 1])
         if tiles == OUTER:
             pl.when(is_bottom)(lambda: pl.semaphore_wait(barrier, 3))
-            pl.when(not_bottom)(lambda: pl.semaphore_wait(barrier, 4))
+            pl.when(not_bottom & (lat != lats - 2))(lambda: pl.semaphore_wait(barrier, 4))
+            pl.when(is_relay)(lambda: pl.semaphore_wait(barrier, 5))
             for index in range(len(GROUPS)):
                 send_lat(0, index)
     for part in range(3):
@@ -236,76 +269,115 @@
     def at(step, f, level, tile, shift=0):
         return cur[step, f, level, pl.ds(TOP + 8 * tile + shift, 8), :]
 
-    def spread_edges(tiles, fields):
+    def split(value):
+        high = value.astype(jnp.bfloat16)
+        low = (value - high.astype(jnp.float32)).astype(jnp.bfloat16)
+        return jnp.concatenate([high, low], axis=1)
+
+    def along(step, tiles):
+        flat = (8 * X_LEVELS, COLS)
         for tile in tiles:
-            for f in fields:
-                packed = halo[f, tile]
+            rows = pl.ds(TOP + 8 * tile, 8)
+            turned = jnp.broadcast_to(coriolis(tile)[None], (X_LEVELS, 8, COLS)).reshape(flat)
+
+            def some(i, total):
+                levels = pl.ds(i * X_LEVELS, X_LEVELS)
+                value = [cur[step, f, levels, rows, :].reshape(flat) for f in range(FIELDS)]
+                mixed = jnp.dot(
+                    jnp.concatenate([split(v) for v in value], axis=0),
+                    filters[:, : 2 * COLS],
+                    preferred_element_type=jnp.float32,
+                )
+                half = jnp.dot(
+                    split(0.02 * value[1] - 0.005 * value[0]),
+                    filters[:, 2 * COLS :],
+                    preferred_element_type=jnp.float32,
+                )
+                middles = []
+                for place in range(X_LEVELS):
+                    part = half[8 * place : 8 * place + 8]
+                    middles.append(total + part)
+                    total = middles[-1] + part
+                speed = value[2] * (1.0 / 60.0)
+                for f in range(FIELDS):
+                    both = mixed[flat[0] * f : flat[0] * (f + 1)]
+                    grown = (1.6 * value[f] + 0.1 * both[:, :COLS]) - speed * both[:, COLS:]
+                    if f == 2:
+                        grown = grown + (turned * value[3] - jnp.concatenate(middles, axis=0))
+                    if f == 3:
+                        grown = grown - turned * value[2]
+                    grown = grown.reshape(X_LEVELS, 8, COLS)
+                    if step == 0:
+                        cur[1, f, levels, rows, :] = grown
+                    else:
+                        result[f, levels, pl.ds(8 * tile, 8), :] = grown
+                return total
+
+            lax.fori_loop(0, LEVELS // X_LEVELS, some, zero)
+
+    def repair(step, tiles):
+        at_126, at_127, at_0 = quarter == 0, quarter == 1, quarter == 2
+        at_edge = (lane < 2) | (lane >= COLS - 2)
+        for tile in tiles:
+            speed = own[step, 2, tile] * (1.0 / 60.0)
+            gap = [halo[f, tile] - own[step, f, tile] for f in range(FIELDS)]
+            change = []
+            for f in range(FIELDS):
+                back_1, on_1 = pltpu.roll(gap[f], COLS - 1, 1), pltpu.roll(gap[f], 1, 1)
+                back_2, on_2 = pltpu.roll(gap[f], COLS - 2, 1), pltpu.roll(gap[f], 2, 1)
+                near = jnp.where(at_127, back_1, jnp.where(at_0, on_1, 0.0))
+                far = jnp.where(
+                    at_126,
+                    -back_2,
+                    jnp.where(at_127, 8.0 * back_1 - back_2, jnp.where(at_0, on_2 - 8.0 * on_1, on_2)),
+                )
+                change.append(0.1 * near - speed * far)
+            dense = 0.02 * gap[1] - 0.005 * gap[0]
+            half = jnp.where(
+                at_127, pltpu.roll(dense, COLS - 1, 1), jnp.where(at_0, -pltpu.roll(dense, 1, 1), 0.0)
+            )
+            total = half
+            for shift in (4, 8, 16, 32, 64):
+                total = total + jnp.where(lane >= shift, pltpu.roll(total, shift, 1), 0.0)
+            change[2] = change[2] - (2.0 * total - half)
+            for f in range(FIELDS):
                 for level in range(LEVELS):
-                    edges[f, level, pl.ds(8 * tile, 8), :] = turn_lanes(packed, 126 - 4 * level)
-
-    def sweep(step, tiles, fields, axis, last, unroll):
+                    edges[f, level, pl.ds(8 * tile, 8), :] = jnp.where(
+                        at_edge, turn_lanes(change[f], 126 - 4 * level), 0.0
+                    )
+
+    def sweep(step, tiles, fields, unroll):
         units = [(tile, f) for tile in tiles for f in fields]
-        forces = [tile for tile in tiles if 2 + axis in fields]
-        turned = {tile: coriolis(tile) for tile in tiles} if axis == 0 else None
+        forces = [tile for tile in tiles if 3 in fields]
 
         def one(level, parts_done, sums):
             for tile in tiles:
-                near = {}
-
-                def value(f):
-                    if (f, 0) not in near:
-                        near[f, 0] = at(step, f, level, tile)
-                    return near[f, 0]
-
-                def edge(f):
-                    if (f, 1) not in near:
-                        near[f, 1] = edges[f, level, pl.ds(8 * tile, 8), :]
-                    return near[f, 1]
-
-                def sides(f):
-                    if (f, 2) not in near:
-                        if axis == 0:
-                            near[f, 2] = (
-                                pltpu.roll(jnp.where(lane_0, edge(f), value(f)), COLS - 1, 1),
-                                pltpu.roll(jnp.where(lane_127, edge(f), value(f)), 1, 1),
-                            )
-                        else:
-                            near[f, 2] = at(step, f, level, tile, 1), at(step, f, level, tile, -1)
-                    return near[f, 2]
-
-                def far_sides(f):
-                    if axis == 0:
-                        return (
-                            pltpu.roll(jnp.where(lane_1, edge(f), value(f)), COLS - 2, 1),
-                            pltpu.roll(jnp.where(lane_126, edge(f), value(f)), 2, 1),
-                        )
-                    return at(step, f, level, tile, 2), at(step, f, level, tile, -2)
-
-                speed = value(2 + axis) * (1.0 / 60.0)
+                sides = {}
+
+                def beside(f):
+                    if f not in sides:
+                        sides[f] = at(step, f, level, tile, 1), at(step, f, level, tile, -1)
+                    return sides[f]
+
+                speed = at(step, 3, level, tile) * (1.0 / 60.0)
                 speed_8 = 8.0 * speed
                 to_plus, to_minus = 0.1 - speed_8, 0.1 + speed_8
+                pivots = pivot[level, pl.ds(8 * tile, 8), :]
                 for f in fields:
-                    plus, minus = sides(f)
-                    plus_2, minus_2 = far_sides(f)
-                    total = (plus * to_plus + minus * to_minus) + (plus_2 - minus_2) * speed
-                    if axis == 0:
-                        total = total + 1.6 * value(f)
-                        if f == 2:
-                            total = total + turned[tile] * value(3)
-                        if f == 3:
-                            total = total - turned[tile] * value(2)
-                    if f == 2 + axis:
-                        plus_t, minus_t = sides(0)
-                        plus_s, minus_s = sides(1)
+                    plus, minus = beside(f)
+                    gap = at(step, f, level, tile, 2) - at(step, f, level, tile, -2)
+                    total = (plus * to_plus + minus * to_minus) + gap * speed
+                    if f == 3:
+                        plus_t, minus_t = beside(0)
+                        plus_s, minus_s = beside(1)
                         half = 0.02 * (plus_s - minus_s) - 0.005 * (plus_t - minus_t)
                         middle = sums[tile] + half
                         sums[tile] = middle + half
                         total = total - middle
                     ref = grow(step, f, level, tile)
-                    if last:
-                        pivots = pivot[level, pl.ds(8 * tile, 8), :]
-                        total = pivots * ((total + ref[...]) + parts_done[tile, f])
-                        parts_done[tile, f] = total
+                    known = ref[...] + edges[f, level, pl.ds(8 * tile, 8), :]
+                    total = pivots * ((total + known) + parts_done[tile, f])
+                    parts_done[tile, f] = total
                     ref[...] = total
 
         def some(i, carry):
@@ -313,10 +385,9 @@
             sums = dict(zip(forces, carry[1]))
             for place in range(unroll):
                 one(i * unroll + place, parts_done, sums)
-            return tuple(parts_done[u] for u in units) if last else (), tuple(sums[k] for k in forces)
-
-        start = ((zero,) * len(units) if last else (), (zero,) * len(forces))
-        repeat(LEVELS // unroll, some, start)
+            return tuple(parts_done[u] for u in units), tuple(sums[k] for k in forces)
+
+        repeat(LEVELS // unroll, some, ((zero,) * len(units), (zero,) * len(forces)))
 
     def substitute(step, tiles, fields, unroll):
         units = [(tile, f) for tile in tiles for f in fields]
@@ -344,21 +415,26 @@
         for tile in tiles:
             pack_lon(1, tile, pair, packs[tile, 2 * pair], packs[tile, 2 * pair + 1])
 
-    sweep(0, INNER, every, 1, False, 2)
+    along(0, OUTER)
+    along(0, INNER)
     for part in range(3):
         wait_lon(0, part)
-    spread_edges(OUTER, every)
-    sweep(0, OUTER, every, 0, False, X_UNROLL)
-    spread_edges(INNER, every)
-    sweep(0, INNER, every, 0, True, X_UNROLL)
+    repair(0, OUTER)
+    hand_on(0, 0)
+    repair(0, INNER)
+    sweep(0, INNER, every, 2)
+    hand_on(0, 1)
     packs = substitute(0, INNER, every, 8)
     for pair in range(2):
         pack_next(INNER, pair, packs)
     send_lon_part(1, 0)
+    hand_on(0, 2)
     packs = {}
     for index, group in enumerate(GROUPS):
         wait_lat(0, index)
-        sweep(0, OUTER, group, 1, True, Y_UNROLL)
+        if index == 1:
+            hand_on(0, 3)
+        sweep(0, OUTER, group, Y_UNROLL)
         packs.update(substitute(0, OUTER, group, 16))
         send_lat(1, index)
         for pair in range(2):
@@ -366,25 +442,27 @@
                 pack_next(OUTER, pair, packs)
                 send_lon_part(1, 1 + pair)
 
-    sweep(1, INNER, every, 1, False, 2)
+    along(1, INNER)
     wait_lon(1, 0)
-    spread_edges(INNER, every)
-    sweep(1, INNER, every, 0, True, X_UNROLL)
+    repair(1, INNER)
+    sweep(1, INNER, every, 2)
     substitute(1, INNER, every, 8)
+    along(1, OUTER)
     for part in (1, 2):
         wait_lon(1, part)
-    spread_edges(OUTER, every)
-    sweep(1, OUTER, every, 0, False, X_UNROLL)
+    repair(1, OUTER)
     for index, group in enumerate(GROUPS):
         wait_lat(1, index)
-        sweep(1, OUTER, group, 1, True, Y_UNROLL)
+        hand_on(1, index)
+        sweep(1, OUTER, group, Y_UNROLL)
         substitute(1, OUTER, group, 16)
 
     for step in range(2):
         for index in range(len(GROUPS)):
-            up, across, down = lat_copies(step, index)
+            up, _, down, onward = lat_copies(step, index)
             up.wait_send()
             pl.when(not_bottom)(lambda: down.wait_send())
+            pl.when(is_relay)(lambda: onward.wait_send())
         for part in range(3):
             for copy in lon_copies(step, part):
                 copy.wait_send()
@@ -406,9 +484,12 @@
             pltpu.VMEM((2, 2, 4, 2, 8, COLS), jnp.float32),
             pltpu.VMEM((FIELDS, 4, 8, COLS), jnp.float32),
             pltpu.VMEM((FIELDS, LEVELS, ROWS, COLS), jnp.float32),
+            pltpu.VMEM((2, FIELDS, LEVELS, 8, COLS), jnp.float32),
+            pltpu.VMEM((2, FIELDS, 4, 8, COLS), jnp.float32),
+            pltpu.VMEM((2 * COLS, 3 * COLS), jnp.bfloat16),
             pltpu.SemaphoreType.DMA((6,)),
-            pltpu.SemaphoreType.DMA((2, 2, groups)),
-            pltpu.SemaphoreType.DMA((2, 2, groups)),
+            pltpu.SemaphoreType.DMA((3, 2, groups)),
+            pltpu.SemaphoreType.DMA((3, 2, groups)),
             pltpu.SemaphoreType.DMA((2, 2, 3)),
             pltpu.SemaphoreType.DMA((2, 2, 3)),
         ],

time: 33.7 us -> 31.5 us (0.935)
  Pallas kernels: 32.2 us -> 30 us
    pallas_call x1, Pallas kernels: 32.2 us -> 30 us  [per_device(): pl.pallas_call(functools.partial(kernel, lons, lats), out_shape=jax.Shape...]
where the time goes in v4:
time: 31.5 us; the launch traced here: 31.3 us
  Pallas kernels  30 us (95%)
  local copies, waits for them, and re-layouts  1.32 us (4%)
    pallas_call x1, Pallas kernels, per_device(): pl.pallas_call(functools.partial(kernel, lons, lats), out_shape=jax.Shape...  30 us
    unnamed x1, local copies, waits for them, and re-layouts  1.32 us

profile of v4, /device:TPU:14, one launch (start us, length us, event | category | flops | bytes accessed | tf_op | source)
XLA Modules:
  0.0 31.3 jit_solution(13677067932145149985)
XLA Ops:
  0.0 30.0 %ocean_steps.1 = f32[4,32,32,128]{3,2,1,0:T(8,128)S(1)} custom-call(f32[4,32,32,128]{3,2,1,0:T(8,128)} %state_ref.1, s32[32,128]{1,0:T(8,128)} %land_ref.1, s32[32,128]{1,0:T(8,128)} %depth_ref.1), custom_call_target="tpu_custom_call" | custom-call | tf_op jit(solution)/shard_map/ocean_steps/pallas_call | solution.py:474
  30.0 1.3 %copy.5 = f32[4,32,32,128]{3,2,1,0:T(8,128)} copy(f32[4,32,32,128]{3,2,1,0:T(8,128)S(1)} %ocean_steps.1) | data formatting | bytes 4194304

commit v5 on v4

--- a/solution.py
+++ b/solution.py
@@ -11,7 +11,7 @@
 FIELDS, LEVELS, ROWS, COLS = 4, 32, 32, 128
 TOP = 8
 DEPTH = 48
-GROUPS = ((0,), (1,), (2,), (3,))
+GROUPS = ((0, 1), (2, 3))
 INNER, OUTER = (1, 2), (0, 3)
 SLOT = {1: 0, 2: 1, 0: 2, 3: 3}
 COVER = 8
@@ -34,18 +34,16 @@
 
 def kernel(
     lons, lats, state_ref, land_ref, depth_ref, result,
-    cur, pivot, mask, send_lon, recv_lon, halo, edges, relayed, own, filters,
+    cur, pivot, mask, send_lon, recv_lon, halo, edges, own, filters,
     load_sem, lat_send, lat_recv, lon_send, lon_recv,
 ):
     lon, lat = lax.axis_index("lon"), lax.axis_index("lat")
     west = {"lon": lax.rem(lon + lons - 1, lons)}
     east = {"lon": lax.rem(lon + 1, lons)}
     north, south = {"lat": lat + 1}, {"lat": lat - 1}
-    relay = {"lon": lons - 1 - lon, "lat": lat - 1}
-    origin = {"lon": lons - 1 - lon, "lat": lat + 1}
+    fold = {"lon": lons - 1 - lon}
     is_top, is_bottom = lat == lats - 1, lat == 0
     not_top, not_bottom = lat < lats - 1, lat > 0
-    is_relay = lat == lats - 2
 
     barrier = pltpu.get_barrier_semaphore()
 
@@ -55,18 +53,19 @@
     greet(west)
     greet(east)
     pl.when(not_top)(lambda: greet(north))
-    pl.when(is_top)(lambda: greet(relay))
-    pl.when(is_relay)(lambda: greet(origin))
+    pl.when(is_top)(lambda: greet(fold))
     pl.when(not_bottom)(lambda: greet(south))
 
     loads = [
-        pltpu.make_async_copy(land_ref, mask.at[0], load_sem.at[4]),
-        pltpu.make_async_copy(depth_ref, mask.at[1], load_sem.at[5]),
+        pltpu.make_async_copy(land_ref, mask.at[0], load_sem.at[3]),
+        pltpu.make_async_copy(depth_ref, mask.at[1], load_sem.at[4]),
     ] + [
         pltpu.make_async_copy(
-            state_ref.at[f], cur.at[0, f, :, pl.ds(TOP, ROWS)], load_sem.at[f]
+            state_ref.at[:, :, pl.ds(8 * first, 8 * count)],
+            cur.at[0, :, :, pl.ds(TOP + 8 * first, 8 * count)],
+            load_sem.at[at_load],
         )
-        for f in range(FIELDS)
+        for at_load, (first, count) in enumerate(((0, 1), (3, 1), (1, 2)))
     ]
     for load in loads:
         load.start()
@@ -76,19 +75,6 @@
     quarter = lax.rem(lane, 4)
     low_pair = quarter < 2
     group_lane = lane // 4
-
-    source = lax.broadcasted_iota(jnp.int32, (COLS, COLS), 0)
-    offset = lax.rem(source - lax.broadcasted_iota(jnp.int32, (COLS, COLS), 1) + COLS, COLS)
-
-    def weigh(plus, minus, plus_2, minus_2):
-        weights = jnp.where(offset == 1, plus, jnp.where(offset == COLS - 1, minus, 0.0))
-        weights = jnp.where(offset == 2, plus_2, jnp.where(offset == COLS - 2, minus_2, weights))
-        return weights.astype(jnp.bfloat16)
-
-    for at_filter, taps in enumerate(((1.0, 1.0, 0.0, 0.0), (8.0, -8.0, -1.0, 1.0), (1.0, -1.0, 0.0, 0.0))):
-        weights = weigh(*taps)
-        for half in range(2):
-            filters[pl.ds(COLS * half, COLS), pl.ds(COLS * at_filter, COLS)] = weights
 
     def coriolis(tile):
         row = (lat * ROWS + tile * 8 + sublane).astype(jnp.float32)
@@ -104,19 +90,6 @@
 
         lax.fori_loop(0, LEVELS, clear, 0)
 
-    loads[0].wait()
-    loads[1].wait()
-    inside, last = factors()
-    wet_count = []
-    for tile in range(4):
-        rows = pl.ds(8 * tile, 8)
-        count = jnp.where(mask[0, rows, :] == 1, mask[1, rows, :], 0)
-        wet_count.append(count)
-        for level in range(LEVELS):
-            pivot[level, rows, :] = jnp.where(
-                count > level + 1, inside[level], jnp.where(count == level + 1, last[level], 0.0)
-            )
-
     def lat_copies(step, index):
         group = GROUPS[index]
         fields = pl.ds(group[0], len(group))
@@ -126,9 +99,7 @@
 
         up = (rows(TOP + ROWS - 2), rows(TOP - 2))
         down = (rows(TOP), rows(TOP + ROWS))
-        held = relayed.at[step, fields, :, pl.ds(0, 2)]
-        across = (rows(TOP + ROWS - 2), held)
-        onward = (held, rows(TOP + ROWS))
+        across = (rows(TOP + ROWS - 2), rows(TOP + ROWS))
 
         def remote(pair, send_sem, recv_sem, device):
             return pltpu.make_async_remote_copy(
@@ -142,51 +113,49 @@
 
         return (
             remote(up, lat_send.at[0], lat_recv.at[0], north),
-            remote(across, lat_send.at[0], lat_recv.at[2], relay),
+            remote(across, lat_send.at[0], lat_recv.at[1], fold),
             remote(down, lat_send.at[1], lat_recv.at[1], south),
-            remote(onward, lat_send.at[2], lat_recv.at[1], north),
         )
 
-    def send_lat(step, index):
-        up, across, down, _ = lat_copies(step, index)
+    def send_up(step, index):
+        up, across, _ = lat_copies(step, index)
         pl.when(not_top)(lambda: up.start())
         pl.when(is_top)(lambda: across.start())
+
+    def send_down(step, index):
+        down = lat_copies(step, index)[2]
         pl.when(not_bottom)(lambda: down.start())
 
-    def hand_on(step, index):
-        _, across, _, onward = lat_copies(step, index)
-
-        @pl.when(is_relay)
-        def _():
-            across.wait_recv()
-            onward.start()
-
-    def wait_lat(step, index):
-        up, _, down, _ = lat_copies(step, index)
-        down.wait_recv()
+    def wait_below(step, index):
+        up = lat_copies(step, index)[0]
         pl.when(not_bottom)(lambda: up.wait_recv())
+
+    def wait_above(step, index):
+        lat_copies(step, index)[2].wait_recv()
 
         @pl.when(is_top)
         def _():
-            reverse = (COLS - 1) - lax.broadcasted_iota(jnp.int32, (2, COLS), 1)
-
-            for level in range(LEVELS):
-                for f in GROUPS[index]:
-                    got = cur[step, f, level, pl.ds(TOP + ROWS, 2), :]
-                    got = jnp.take_along_axis(got, reverse, axis=1)
-                    sign = 1.0 if f < 2 else -1.0
-                    cur[step, f, level, pl.ds(TOP + ROWS, 1), :] = sign * got[1:2]
-                    cur[step, f, level, pl.ds(TOP + ROWS + 1, 1), :] = sign * got[0:1]
-
-    parts = ((pl.ds(0, 2), pl.ds(0, 2)), (pl.ds(2, 2), pl.ds(0, 1)), (pl.ds(2, 2), pl.ds(1, 1)))
+            reverse = (COLS - 1) - lane
+            flat = cur.reshape(2, FIELDS, LEVELS * DEPTH, COLS)
+            for f in GROUPS[index]:
+                for first in range(0, LEVELS, 8):
+                    places = [pl.ds(first * DEPTH + TOP + ROWS + m, 8, stride=DEPTH) for m in range(2)]
+                    got = [flat[step, f, place, :] for place in places]
+                    got = [jnp.take_along_axis(value, reverse, axis=1) for value in got]
+                    if f >= 2:
+                        got = [-value for value in got]
+                    flat[step, f, places[0], :] = got[1]
+                    flat[step, f, places[1], :] = got[0]
+
+    parts = ((pl.ds(0, 2), INNER), (pl.ds(2, 1), (0,)), (pl.ds(3, 1), (3,)))
 
     def lon_copies(step, part):
-        tiles, pairs = parts[part]
+        slots = parts[part][0]
 
         def remote(side, device):
             return pltpu.make_async_remote_copy(
-                src_ref=send_lon.at[step, side, tiles, pairs],
-                dst_ref=recv_lon.at[step, side, tiles, pairs],
+                src_ref=send_lon.at[step, side, slots],
+                dst_ref=recv_lon.at[step, side, slots],
                 send_sem=lon_send.at[step, side, part],
                 recv_sem=lon_recv.at[step, side, part],
                 device_id=device,
@@ -209,10 +178,8 @@
     def wait_lon(step, part):
         for copy in lon_copies(step, part):
             copy.wait_recv()
-        tiles = INNER if part == 0 else OUTER
-        pairs = (0, 1) if part == 0 else (part - 1,)
-        for tile in tiles:
-            for pair in pairs:
+        for tile in parts[part][1]:
+            for pair in range(2):
                 from_west = recv_lon[step, 0, SLOT[tile], pair]
                 from_east = recv_lon[step, 1, SLOT[tile], pair]
                 halo[2 * pair, tile] = jnp.where(low_pair, from_west, pltpu.roll(from_east, 2, 1))
@@ -229,37 +196,79 @@
 
     zero = jnp.zeros((8, COLS), jnp.float32)
 
-    for load in loads[2:]:
-        load.wait()
-    first_packs = {}
-    for tiles in (OUTER, INNER):
-        def cover(i, packs):
-            packs = list(packs)
+    loads[0].wait()
+    loads[1].wait()
+    wet_count = [
+        jnp.where(mask[0, pl.ds(8 * tile, 8), :] == 1, mask[1, pl.ds(8 * tile, 8), :], 0)
+        for tile in range(4)
+    ]
+
+    def cover(tiles):
+        def some(i, carry):
             for place in range(COVER):
                 level = i * COVER + place
-                at = 0
                 for tile in tiles:
                     wet = wet_count[tile] > level
                     for f in range(FIELDS):
                         rows = pl.ds(TOP + 8 * tile, 8)
-                        value = jnp.where(wet, cur[0, f, level, rows, :], 0.0)
-                        cur[0, f, level, rows, :] = value
-                        packs[at] = collect(place, value, packs[at])
-                        at += 1
+                        cur[0, f, level, rows, :] = jnp.where(wet, cur[0, f, level, rows, :], 0.0)
+            return carry
+
+        lax.fori_loop(0, LEVELS // COVER, some, 0)
+
+    def pack_first(tiles):
+        units = [(tile, f) for tile in tiles for f in range(FIELDS)]
+
+        def some(i, packs):
+            packs = list(packs)
+            for place in range(COVER):
+                for at_unit, (tile, f) in enumerate(units):
+                    value = cur[0, f, i * COVER + place, pl.ds(TOP + 8 * tile, 8), :]
+                    packs[at_unit] = collect(place, value, packs[at_unit])
             return tuple(turn_lanes(pack, -4 * COVER) for pack in packs)
 
-        packs = repeat(LEVELS // COVER, cover, (zero,) * (4 * len(tiles)))
+        packs = lax.fori_loop(0, LEVELS // COVER, some, (zero,) * len(units))
         for i, tile in enumerate(tiles):
             for pair in range(2):
                 pack_lon(0, tile, pair, packs[4 * i + 2 * pair], packs[4 * i + 2 * pair + 1])
-        if tiles == OUTER:
-            pl.when(is_bottom)(lambda: pl.semaphore_wait(barrier, 3))
-            pl.when(not_bottom & (lat != lats - 2))(lambda: pl.semaphore_wait(barrier, 4))
-            pl.when(is_relay)(lambda: pl.semaphore_wait(barrier, 5))
-            for index in range(len(GROUPS)):
-                send_lat(0, index)
-    for part in range(3):
-        send_lon_part(0, part)
+
+    loads[2].wait()
+    loads[3].wait()
+    cover(OUTER)
+    pl.when(is_bottom)(lambda: pl.semaphore_wait(barrier, 3))
+    pl.when(not_bottom)(lambda: pl.semaphore_wait(barrier, 4))
+    for index in range(len(GROUPS)):
+        send_up(0, index)
+    loads[4].wait()
+    cover(INNER)
+    pack_first(INNER)
+    send_lon_part(0, 0)
+    pack_first(OUTER)
+    send_lon_part(0, 1)
+    send_lon_part(0, 2)
+    for index in range(len(GROUPS)):
+        send_down(0, index)
+
+    inside, last = factors()
+    for tile in range(4):
+        count = wet_count[tile]
+        for level in range(LEVELS):
+            pivot[level, pl.ds(8 * tile, 8), :] = jnp.where(
+                count > level + 1, inside[level], jnp.where(count == level + 1, last[level], 0.0)
+            )
+
+    source = lax.broadcasted_iota(jnp.int32, (COLS, COLS), 0)
+    offset = lax.rem(source - lax.broadcasted_iota(jnp.int32, (COLS, COLS), 1) + COLS, COLS)
+
+    def weigh(plus, minus, plus_2, minus_2):
+        weights = jnp.where(offset == 1, plus, jnp.where(offset == COLS - 1, minus, 0.0))
+        weights = jnp.where(offset == 2, plus_2, jnp.where(offset == COLS - 2, minus_2, weights))
+        return weights.astype(jnp.bfloat16)
+
+    for at_filter, taps in enumerate(((1.0, 1.0, 0.0, 0.0), (8.0, -8.0, -1.0, 1.0), (1.0, -1.0, 0.0, 0.0))):
+        weights = weigh(*taps)
+        for half in range(2):
+            filters[pl.ds(COLS * half, COLS), pl.ds(COLS * at_filter, COLS)] = weights
 
     def grow(step, f, level, tile):
         if step == 0:
@@ -411,58 +420,52 @@
 
     every = tuple(range(FIELDS))
 
-    def pack_next(tiles, pair, packs):
+    def pack_next(tiles, packs):
         for tile in tiles:
-            pack_lon(1, tile, pair, packs[tile, 2 * pair], packs[tile, 2 * pair + 1])
+            for pair in range(2):
+                pack_lon(1, tile, pair, packs[tile, 2 * pair], packs[tile, 2 * pair + 1])
+
+    def outer(step, tile, wait, send):
+        packs = {}
+        for index, group in enumerate(GROUPS):
+            wait(step, index)
+            sweep(step, (tile,), group, Y_UNROLL)
+            packs.update(substitute(step, (tile,), group, 16))
+            if step == 0:
+                send(1, index)
+        if step == 0:
+            pack_next((tile,), packs)
+            send_lon_part(1, 1 if tile == 0 else 2)
 
     along(0, OUTER)
     along(0, INNER)
     for part in range(3):
         wait_lon(0, part)
+    repair(0, INNER)
+    sweep(0, INNER, every, 4)
+    pack_next(INNER, substitute(0, INNER, every, 8))
+    send_lon_part(1, 0)
     repair(0, OUTER)
-    hand_on(0, 0)
-    repair(0, INNER)
-    sweep(0, INNER, every, 2)
-    hand_on(0, 1)
-    packs = substitute(0, INNER, every, 8)
-    for pair in range(2):
-        pack_next(INNER, pair, packs)
-    send_lon_part(1, 0)
-    hand_on(0, 2)
-    packs = {}
-    for index, group in enumerate(GROUPS):
-        wait_lat(0, index)
-        if index == 1:
-            hand_on(0, 3)
-        sweep(0, OUTER, group, Y_UNROLL)
-        packs.update(substitute(0, OUTER, group, 16))
-        send_lat(1, index)
-        for pair in range(2):
-            if group[-1] == 2 * pair + 1:
-                pack_next(OUTER, pair, packs)
-                send_lon_part(1, 1 + pair)
-
     along(1, INNER)
+    outer(0, 0, wait_below, send_down)
+    outer(0, 3, wait_above, send_up)
+
     wait_lon(1, 0)
     repair(1, INNER)
-    sweep(1, INNER, every, 2)
+    sweep(1, INNER, every, 4)
     substitute(1, INNER, every, 8)
     along(1, OUTER)
-    for part in (1, 2):
-        wait_lon(1, part)
+    wait_lon(1, 1)
+    wait_lon(1, 2)
     repair(1, OUTER)
-    for index, group in enumerate(GROUPS):
-        wait_lat(1, index)
-        hand_on(1, index)
-        sweep(1, OUTER, group, Y_UNROLL)
-        substitute(1, OUTER, group, 16)
+    outer(1, 0, wait_below, None)
+    outer(1, 3, wait_above, None)
 
     for step in range(2):
         for index in range(len(GROUPS)):
-            up, _, down, onward = lat_copies(step, index)
+            up, _, down = lat_copies(step, index)
             up.wait_send()
             pl.when(not_bottom)(lambda: down.wait_send())
-            pl.when(is_relay)(lambda: onward.wait_send())
         for part in range(3):
             for copy in lon_copies(step, part):
                 copy.wait_send()
@@ -484,12 +487,11 @@
             pltpu.VMEM((2, 2, 4, 2, 8, COLS), jnp.float32),
             pltpu.VMEM((FIELDS, 4, 8, COLS), jnp.float32),
             pltpu.VMEM((FIELDS, LEVELS, ROWS, COLS), jnp.float32),
-            pltpu.VMEM((2, FIELDS, LEVELS, 8, COLS), jnp.float32),
             pltpu.VMEM((2, FIELDS, 4, 8, COLS), jnp.float32),
             pltpu.VMEM((2 * COLS, 3 * COLS), jnp.bfloat16),
-            pltpu.SemaphoreType.DMA((6,)),
-            pltpu.SemaphoreType.DMA((3, 2, groups)),
-            pltpu.SemaphoreType.DMA((3, 2, groups)),
+            pltpu.SemaphoreType.DMA((5,)),
+            pltpu.SemaphoreType.DMA((2, 2, groups)),
+            pltpu.SemaphoreType.DMA((2, 2, groups)),
             pltpu.SemaphoreType.DMA((2, 2, 3)),
             pltpu.SemaphoreType.DMA((2, 2, 3)),
         ],

time: 31.5 us -> 30.5 us (0.968)
  Pallas kernels: 30 us -> 29 us
    pallas_call x1, Pallas kernels: 30 us -> 29 us  [per_device(): pl.pallas_call(functools.partial(kernel, lons, lats), out_shape=jax.Shape...]
where the time goes in v5:
time: 30.5 us; the launch traced here: 30.4 us
  Pallas kernels  29 us (95%)
  local copies, waits for them, and re-layouts  1.32 us (4%)
    pallas_call x1, Pallas kernels, per_device(): pl.pallas_call(functools.partial(kernel, lons, lats), out_shape=jax.Shape...  29 us
    unnamed x1, local copies, waits for them, and re-layouts  1.32 us

profile of v5, /device:TPU:14, one launch (start us, length us, event | category | flops | bytes accessed | tf_op | source)
XLA Modules:
  0.0 30.4 jit_solution(4243068630195994785)
XLA Ops:
  0.0 29.0 %ocean_steps.1 = f32[4,32,32,128]{3,2,1,0:T(8,128)S(1)} custom-call(f32[4,32,32,128]{3,2,1,0:T(8,128)} %state_ref.1, s32[32,128]{1,0:T(8,128)} %land_ref.1, s32[32,128]{1,0:T(8,128)} %depth_ref.1), custom_call_target="tpu_custom_call" | custom-call | tf_op jit(solution)/shard_map/ocean_steps/pallas_call | solution.py:477
  29.0 1.3 %copy.5 = f32[4,32,32,128]{3,2,1,0:T(8,128)} copy(f32[4,32,32,128]{3,2,1,0:T(8,128)S(1)} %ocean_steps.1) | data formatting | bytes 4194304

commit v6 on v5

--- a/solution.py
+++ b/solution.py
@@ -32,9 +32,83 @@
     return inside, last
 
 
+def turn_lanes(value, amount):
+    amount = amount % COLS
+    return value if amount == 0 else pltpu.roll(value, amount, 1)
+
+
+def column_work(at, grow, pivot, edges, collect):
+    zero = jnp.zeros((8, COLS), jnp.float32)
+
+    def sweep(step, tiles, fields, unroll):
+        units = [(tile, f) for tile in tiles for f in fields]
+        forces = [tile for tile in tiles if 3 in fields]
+
+        def one(level, parts_done, sums):
+            for tile in tiles:
+                sides = {}
+
+                def beside(f):
+                    if f not in sides:
+                        sides[f] = at(step, f, level, tile, 1), at(step, f, level, tile, -1)
+                    return sides[f]
+
+                speed = at(step, 3, level, tile) * (1.0 / 60.0)
+                speed_8 = 8.0 * speed
+                to_plus, to_minus = 0.1 - speed_8, 0.1 + speed_8
+                pivots = pivot[level, pl.ds(8 * tile, 8), :]
+                for f in fields:
+                    plus, minus = beside(f)
+                    gap = at(step, f, level, tile, 2) - at(step, f, level, tile, -2)
+                    total = (plus * to_plus + minus * to_minus) + gap * speed
+                    if f == 3:
+                        plus_t, minus_t = beside(0)
+                        plus_s, minus_s = beside(1)
+                        half = 0.02 * (plus_s - minus_s) - 0.005 * (plus_t - minus_t)
+                        middle = sums[tile] + half
+                        sums[tile] = middle + half
+                        total = total - middle
+                    source, target = grow(step, f, level, tile)
+                    known = source[...] + edges[f, level, pl.ds(8 * tile, 8), :]
+                    total = pivots * ((total + known) + parts_done[tile, f])
+                    parts_done[tile, f] = total
+                    target[...] = total
+
+        def some(i, carry):
+            parts_done = dict(zip(units, carry[0]))
+            sums = dict(zip(forces, carry[1]))
+            for place in range(unroll):
+                one(i * unroll + place, parts_done, sums)
+            return tuple(parts_done[u] for u in units), tuple(sums[k] for k in forces)
+
+        repeat(LEVELS // unroll, some, ((zero,) * len(units), (zero,) * len(forces)))
+
+    def substitute(step, tiles, fields, unroll):
+        units = [(tile, f) for tile in tiles for f in fields]
+        trips = LEVELS // unroll
+
+        def some(i, carry):
+            values, packs = list(carry[0]), [turn_lanes(pack, 4 * unroll) for pack in carry[1]]
+            for place in reversed(range(unroll)):
+                level = (trips - 1 - i) * unroll + place
+                for at_unit, (tile, f) in enumerate(units):
+                    _, ref = grow(step, f, level, tile)
+                    value = ref[...] + pivot[level, pl.ds(8 * tile, 8), :] * values[at_unit]
+                    ref[...] = value
+                    values[at_unit] = value
+                    if step == 0:
+                        packs[at_unit] = collect(place, value, packs[at_unit])
+            return tuple(values), tuple(packs)
+
+        start = ((zero,) * len(units), (zero,) * (len(units) if step == 0 else 0))
+        return dict(zip(units, repeat(trips, some, start)[1]))
+
+    return sweep, substitute
+
+
 def kernel(
-    lons, lats, state_ref, land_ref, depth_ref, result,
-    cur, pivot, mask, send_lon, recv_lon, halo, edges, own, filters,
+    lons, lats, state_ref, land_ref, depth_ref, result, cur, pivot, edges,
+    mask, send_lon, recv_lon, halo, own, filters,
     load_sem, lat_send, lat_recv, lon_send, lon_recv,
 ):
     lon, lat = lax.axis_index("lon"), lax.axis_index("lat")
@@ -189,10 +263,6 @@
 
     def collect(place, value, packed):
         return jnp.where(group_lane == place, pltpu.roll(value, 4 * place + 2, 1), packed)
-
-    def turn_lanes(value, amount):
-        amount = amount % COLS
-        return value if amount == 0 else pltpu.roll(value, amount, 1)
 
     zero = jnp.zeros((8, COLS), jnp.float32)
 
@@ -272,8 +342,10 @@
 
     def grow(step, f, level, tile):
         if step == 0:
-            return cur.at[1, f, level, pl.ds(TOP + 8 * tile, 8), :]
-        return result.at[f, level, pl.ds(8 * tile, 8), :]
+            ref = cur.at[1, f, level, pl.ds(TOP + 8 * tile, 8), :]
+        else:
+            ref = result.at[f, level, pl.ds(8 * tile, 8), :]
+        return ref, ref
 
     def at(step, f, level, tile, shift=0):
         return cur[step, f, level, pl.ds(TOP + 8 * tile + shift, 8), :]
@@ -355,69 +427,7 @@
                         at_edge, turn_lanes(change[f], 126 - 4 * level), 0.0
                     )
 
-    def sweep(step, tiles, fields, unroll):
-        units = [(tile, f) for tile in tiles for f in fields]
-        forces = [tile for tile in tiles if 3 in fields]
-
-        def one(level, parts_done, sums):
-            for tile in tiles:
-                sides = {}
-
-                def beside(f):
-                    if f not in sides:
-                        sides[f] = at(step, f, level, tile, 1), at(step, f, level, tile, -1)
-                    return sides[f]
-
-                speed = at(step, 3, level, tile) * (1.0 / 60.0)
-                speed_8 = 8.0 * speed
-                to_plus, to_minus = 0.1 - speed_8, 0.1 + speed_8
-                pivots = pivot[level, pl.ds(8 * tile, 8), :]
-                for f in fields:
-                    plus, minus = beside(f)
-                    gap = at(step, f, level, tile, 2) - at(step, f, level, tile, -2)
-                    total = (plus * to_plus + minus * to_minus) + gap * speed
-                    if f == 3:
-                        plus_t, minus_t = beside(0)
-                        plus_s, minus_s = beside(1)
-                        half = 0.02 * (plus_s - minus_s) - 0.005 * (plus_t - minus_t)
-                        middle = sums[tile] + half
-                        sums[tile] = middle + half
-                        total = total - middle
-                    ref = grow(step, f, level, tile)
-                    known = ref[...] + edges[f, level, pl.ds(8 * tile, 8), :]
-                    total = pivots * ((total + known) + parts_done[tile, f])
-                    parts_done[tile, f] = total
-                    ref[...] = total
-
-        def some(i, carry):
-            parts_done = dict(zip(units, carry[0]))
-            sums = dict(zip(forces, carry[1]))
-            for place in range(unroll):
-                one(i * unroll + place, parts_done, sums)
-            return tuple(parts_done[u] for u in units), tuple(sums[k] for k in forces)
-
-        repeat(LEVELS // unroll, some, ((zero,) * len(units), (zero,) * len(forces)))
-
-    def substitute(step, tiles, fields, unroll):
-        units = [(tile, f) for tile in tiles for f in fields]
-        trips = LEVELS // unroll
-
-        def some(i, carry):
-            values, packs = list(carry[0]), [turn_lanes(pack, 4 * unroll) for pack in carry[1]]
-            for place in reversed(range(unroll)):
-                level = (trips - 1 - i) * unroll + place
-                for at_unit, (tile, f) in enumerate(units):
-                    ref = grow(step, f, level, tile)
-                    value = ref[...] + pivot[level, pl.ds(8 * tile, 8), :] * values[at_unit]
-                    ref[...] = value
-                    values[at_unit] = value
-                    if step == 0:
-                        packs[at_unit] = collect(place, value, packs[at_unit])
-            return tuple(values), tuple(packs)
-
-        start = ((zero,) * len(units), (zero,) * (len(units) if step == 0 else 0))
-        return dict(zip(units, repeat(trips, some, start)[1]))
-
+    sweep, substitute = column_work(at, grow, pivot, edges, collect)
     every = tuple(range(FIELDS))
 
     def pack_next(tiles, packs):
@@ -459,7 +469,8 @@
     wait_lon(1, 2)
     repair(1, OUTER)
     outer(1, 0, wait_below, None)
-    outer(1, 3, wait_above, None)
+    for index in range(len(GROUPS)):
+        wait_above(1, index)
 
     for step in range(2):
         for index in range(len(GROUPS)):
@@ -471,22 +482,52 @@
                 copy.wait_send()
 
 
+def finish(result, cur, pivot, edges, out_ref, fresh, out_sem):
+    tile = 3
+    copies = [
+        pltpu.make_async_copy(
+            result.at[f, :, pl.ds(0, 8 * tile)], out_ref.at[f, :, pl.ds(0, 8 * tile)], out_sem.at[f]
+        )
+        for f in range(FIELDS)
+    ]
+    for copy in copies:
+        copy.start()
+
+    def at(step, f, level, tile, shift=0):
+        return cur[step, f, level, pl.ds(TOP + 8 * tile + shift, 8), :]
+
+    def grow(step, f, level, tile):
+        return result.at[f, level, pl.ds(8 * tile, 8), :], fresh.at[f, level]
+
+    sweep, substitute = column_work(at, grow, pivot, edges, None)
+    for index, group in enumerate(GROUPS):
+        sweep(1, (tile,), group, Y_UNROLL)
+        substitute(1, (tile,), group, 16)
+        fields = pl.ds(group[0], len(group))
+        copy = pltpu.make_async_copy(
+            fresh.at[fields], out_ref.at[fields, :, pl.ds(8 * tile, 8)], out_sem.at[FIELDS + index]
+        )
+        copy.start()
+        copies.append(copy)
+    for copy in copies:
+        copy.wait()
+
+
 def per_device(lons, lats, state, land_mask, wet_levels):
-    any_spec = pl.BlockSpec(memory_space=pl.ANY)
     groups = len(GROUPS)
-    return pl.pallas_call(
+    block = (FIELDS, LEVELS, ROWS, COLS)
+    kept = (block, (2, FIELDS, LEVELS, DEPTH, COLS), (LEVELS, ROWS, COLS), block)
+    in_vmem = pl.BlockSpec(memory_space=pltpu.VMEM)
+    grown = pl.pallas_call(
         functools.partial(kernel, lons, lats),
-        out_shape=jax.ShapeDtypeStruct(state.shape, jnp.float32),
+        out_shape=[jax.ShapeDtypeStruct(shape, jnp.float32) for shape in kept],
         in_specs=[pl.BlockSpec(memory_space=pltpu.HBM)] * 3,
-        out_specs=pl.BlockSpec(memory_space=pltpu.VMEM),
+        out_specs=[in_vmem] * 4,
         scratch_shapes=[
-            pltpu.VMEM((2, FIELDS, LEVELS, DEPTH, COLS), jnp.float32),
-            pltpu.VMEM((LEVELS, ROWS, COLS), jnp.float32),
             pltpu.VMEM((2, ROWS, COLS), jnp.int32),
             pltpu.VMEM((2, 2, 4, 2, 8, COLS), jnp.float32),
             pltpu.VMEM((2, 2, 4, 2, 8, COLS), jnp.float32),
             pltpu.VMEM((FIELDS, 4, 8, COLS), jnp.float32),
-            pltpu.VMEM((FIELDS, LEVELS, ROWS, COLS), jnp.float32),
             pltpu.VMEM((2, FIELDS, 4, 8, COLS), jnp.float32),
             pltpu.VMEM((2 * COLS, 3 * COLS), jnp.bfloat16),
             pltpu.SemaphoreType.DMA((5,)),
@@ -495,9 +536,23 @@
             pltpu.SemaphoreType.DMA((2, 2, 3)),
             pltpu.SemaphoreType.DMA((2, 2, 3)),
         ],
-        compiler_params=pltpu.CompilerParams(collective_id=0, has_side_effects=True, vmem_limit_bytes=24 * 2**20),
+        compiler_params=pltpu.CompilerParams(
+            collective_id=0, has_side_effects=True, vmem_limit_bytes=24 * 2**20
+        ),
         name="ocean_steps",
     )(*(pltpu.with_memory_space_constraint(x, pltpu.HBM) for x in (state, land_mask, wet_levels)))
+    return pl.pallas_call(
+        finish,
+        out_shape=jax.ShapeDtypeStruct(block, jnp.float32),
+        in_specs=[in_vmem] * 4,
+        out_specs=pl.BlockSpec(memory_space=pltpu.HBM),
+        scratch_shapes=[
+            pltpu.VMEM((FIELDS, LEVELS, 8, COLS), jnp.float32),
+            pltpu.SemaphoreType.DMA((FIELDS + groups,)),
+        ],
+        compiler_params=pltpu.CompilerParams(vmem_limit_bytes=8 * 2**20),
+        name="last_tile",
+    )(*grown)
 
 
 def solution(mesh):

time: 30.5 us -> 30.1 us (0.987)
  local copies, waits for them, and re-layouts: 1.32 us -> 0 us
  Pallas kernels: 29 us -> 29.9 us
    unnamed x1 -> x0, local copies, waits for them, and re-layouts: 1.32 us -> none
    pallas_call x1 -> x2, Pallas kernels: 29 us -> 29.9 us  [the longest x1 28.6 us: per_device(): pl.pallas_call(functools.partial(kernel, lons, lats), out_shape=[jax.Shap...]
where the time goes in v6:
time: 30.1 us; the launch traced here: 29.9 us
  Pallas kernels  29.9 us (99%)
    pallas_call x1, Pallas kernels, per_device(): pl.pallas_call(functools.partial(kernel, lons, lats), out_shape=[jax.Shap...  28.6 us
    pallas_call x1, Pallas kernels, per_device(): pl.pallas_call(finish, out_shape=jax.ShapeDtypeStruct(block, jnp.float32)...  1.36 us

profile of v6, /device:TPU:14, one launch (start us, length us, event | category | flops | bytes accessed | tf_op | source)
XLA Modules:
  0.0 29.9 jit_solution(2839124569849996228)
XLA Ops:
  0.0 28.6 %ocean_steps.1 = (f32[4,32,32,128]{3,2,1,0:T(8,128)S(1)}, f32[2,4,32,48,128]{4,3,2,1,0:T(8,128)S(1)}, f32[32,32,128]{2,1,0:T(8,128)S(1)}, f32[4,32,32,128]{3,2,1,0:T(8,128)S(1)}) custom-call(f32[4,32,32,128]{3,2,1,0:T(8,128)} %state_ref.1, s32[32,128]{1,0:T(8,128)} %land_ref.1, s32[32,128]{1,0:T(8,128)} %depth_ref.1), custom_call_target="tpu_custom_call" | custom-call | tf_op jit(solution)/shard_map/ocean_steps/pallas_call | solution.py:521
  28.6 1.4 %last_tile.1 = f32[4,32,32,128]{3,2,1,0:T(8,128)} custom-call(f32[4,32,32,128]{3,2,1,0:T(8,128)S(1)} %get-tuple-element.9.result, f32[2,4,32,48,128]{4,3,2,1,0:T(8,128)S(1)} %get-tuple-element.10.cur, f32[32,32,128]{2,1,0:T(8,128)S(1)} %get-tuple-element.11.pivot, f32[4,32,32,128]{3,2,1,0:T(8,128)S(1)} %get-tuple-element.12.edges), custom_call_target="tpu_custom_call" | custom-call | tf_op jit(solution)/shard_map/last_tile/pallas_call | solution.py:544

commit v7 on v6

--- a/solution.py
+++ b/solution.py
@@ -11,7 +11,7 @@
 FIELDS, LEVELS, ROWS, COLS = 4, 32, 32, 128
 TOP = 8
 DEPTH = 48
-GROUPS = ((0, 1), (2, 3))
+GROUPS = ((0, 1, 2, 3),)
 INNER, OUTER = (1, 2), (0, 3)
 SLOT = {1: 0, 2: 1, 0: 2, 3: 3}
 COVER = 8

time: 30.1 us -> 30 us (level)
  no operation moved by 1% of the time
where the time goes in v7:
time: 30 us; the launch traced here: 29.8 us
  Pallas kernels  29.8 us (99%)
    pallas_call x1, Pallas kernels, per_device(): pl.pallas_call(functools.partial(kernel, lons, lats), out_shape=[jax.Shap...  28.5 us
    pallas_call x1, Pallas kernels, per_device(): pl.pallas_call(finish, out_shape=jax.ShapeDtypeStruct(block, jnp.float32)...  1.36 us

profile of v7, /device:TPU:14, one launch (start us, length us, event | category | flops | bytes accessed | tf_op | source)
XLA Modules:
  0.0 29.8 jit_solution(4450215605075594708)
XLA Ops:
  0.0 28.5 %ocean_steps.1 = (f32[4,32,32,128]{3,2,1,0:T(8,128)S(1)}, f32[2,4,32,48,128]{4,3,2,1,0:T(8,128)S(1)}, f32[32,32,128]{2,1,0:T(8,128)S(1)}, f32[4,32,32,128]{3,2,1,0:T(8,128)S(1)}) custom-call(f32[4,32,32,128]{3,2,1,0:T(8,128)} %state_ref.1, s32[32,128]{1,0:T(8,128)} %land_ref.1, s32[32,128]{1,0:T(8,128)} %depth_ref.1), custom_call_target="tpu_custom_call" | custom-call | tf_op jit(solution)/shard_map/ocean_steps/pallas_call | solution.py:521
  28.5 1.4 %last_tile.1 = f32[4,32,32,128]{3,2,1,0:T(8,128)} custom-call(f32[4,32,32,128]{3,2,1,0:T(8,128)S(1)} %get-tuple-element.9.result, f32[2,4,32,48,128]{4,3,2,1,0:T(8,128)S(1)} %get-tuple-element.10.cur, f32[32,32,128]{2,1,0:T(8,128)S(1)} %get-tuple-element.11.pivot, f32[4,32,32,128]{3,2,1,0:T(8,128)S(1)} %get-tuple-element.12.edges), custom_call_target="tpu_custom_call" | custom-call | tf_op jit(solution)/shard_map/last_tile/pallas_call | solution.py:544

commit v8 on v6

--- a/solution.py
+++ b/solution.py
@@ -457,8 +457,8 @@
     send_lon_part(1, 0)
     repair(0, OUTER)
     along(1, INNER)
+    outer(0, 3, wait_above, send_up)
     outer(0, 0, wait_below, send_down)
-    outer(0, 3, wait_above, send_up)
 
     wait_lon(1, 0)
     repair(1, INNER)

time: 30.1 us -> 30 us (level)
  no operation moved by 1% of the time
where the time goes in v8:
time: 30 us; the launch traced here: 29.9 us
  Pallas kernels  29.9 us (100%)
    pallas_call x1, Pallas kernels, per_device(): pl.pallas_call(functools.partial(kernel, lons, lats), out_shape=[jax.Shap...  28.5 us
    pallas_call x1, Pallas kernels, per_device(): pl.pallas_call(finish, out_shape=jax.ShapeDtypeStruct(block, jnp.float32)...  1.36 us

profile of v8, /device:TPU:14, one launch (start us, length us, event | category | flops | bytes accessed | tf_op | source)
XLA Modules:
  0.0 29.9 jit_solution(15741478347006343116)
XLA Ops:
  0.0 28.5 %ocean_steps.1 = (f32[4,32,32,128]{3,2,1,0:T(8,128)S(1)}, f32[2,4,32,48,128]{4,3,2,1,0:T(8,128)S(1)}, f32[32,32,128]{2,1,0:T(8,128)S(1)}, f32[4,32,32,128]{3,2,1,0:T(8,128)S(1)}) custom-call(f32[4,32,32,128]{3,2,1,0:T(8,128)} %state_ref.1, s32[32,128]{1,0:T(8,128)} %land_ref.1, s32[32,128]{1,0:T(8,128)} %depth_ref.1), custom_call_target="tpu_custom_call" | custom-call | tf_op jit(solution)/shard_map/ocean_steps/pallas_call | solution.py:521
  28.5 1.4 %last_tile.1 = f32[4,32,32,128]{3,2,1,0:T(8,128)} custom-call(f32[4,32,32,128]{3,2,1,0:T(8,128)S(1)} %get-tuple-element.9.result, f32[2,4,32,48,128]{4,3,2,1,0:T(8,128)S(1)} %get-tuple-element.10.cur, f32[32,32,128]{2,1,0:T(8,128)S(1)} %get-tuple-element.11.pivot, f32[4,32,32,128]{3,2,1,0:T(8,128)S(1)} %get-tuple-element.12.edges), custom_call_target="tpu_custom_call" | custom-call | tf_op jit(solution)/shard_map/last_tile/pallas_call | solution.py:544
